TPU v7x, 32 devices: a whole 2x2x4 slice. The times are simulated.
32 devices in a mesh: dp: 8 (over y, x, core), tensor: 4 (over z).
Axes of the slice: x: 2, y: 2, z: 4, core: 2. Of those that a mesh axis runs over, the one named last changes fastest.
Arguments:
- tokens_in: bfloat16 [16384, 768], P(('dp', 'tensor')), may hold values from -6 to 6
- ln1_gain: float32 [768], replicated, may hold values from 0.25 to 1.75
- ln1_bias: float32 [768], replicated, may hold values from -1.5 to 1.5
- w_qkv: bfloat16 [768, 3, 768], P(None, None, 'tensor'), may hold values from -0.21875 to 0.21875
- b_qkv: float32 [3, 768], P(None, 'tensor'), may hold values from -0.5 to 0.5
- feat_q: bfloat16 [12, 64, 64], P('tensor'), may hold values from -1.5 to 1.5
- feat_k: bfloat16 [12, 64, 64], P('tensor'), may hold values from -1.5 to 1.5
- w_out: bfloat16 [768, 768], P('tensor'), may hold values from -1.75 to 1.75
- b_out: float32 [768], replicated, may hold values from -1.5 to 1.5
- ln2_gain: float32 [768], replicated, may hold values from 0.25 to 1.75
- ln2_bias: float32 [768], replicated, may hold values from -1.5 to 1.5
- w_fc: bfloat16 [768, 3072], P(None, 'tensor'), may hold values from -0.21875 to 0.21875
- b_fc: float32 [3072], P('tensor'), may hold values from -1.5 to 1.5
- w_proj: bfloat16 [3072, 768], P('tensor'), may hold values from -0.109375 to 0.109375
- b_proj: float32 [768], replicated, may hold values from -1.5 to 1.5
- seq_lengths: int32 [8, 2], P('dp'), may hold values from 0 to 2048, as said below
- cotangent: bfloat16 [16384, 768], P(('dp', 'tensor')), may hold values from -6 to 6
Outputs:
- result: bfloat16 [16384, 768], P(('dp', 'tensor'))
- grad_input: bfloat16 [16384, 768], P(('dp', 'tensor'))
- grad_ln1_gain: float32 [768], replicated
- grad_ln1_bias: float32 [768], replicated
- grad_w_qkv: float32 [768, 3, 768], P(None, None, 'tensor')
- grad_b_qkv: float32 [3, 768], P(None, 'tensor')
- grad_feat_q: float32 [12, 64, 64], P('tensor')
- grad_feat_k: float32 [12, 64, 64], P('tensor')
- grad_w_out: float32 [768, 768], P('tensor')
- grad_b_out: float32 [768], replicated
- grad_ln2_gain: float32 [768], replicated
- grad_ln2_bias: float32 [768], replicated
- grad_w_fc: float32 [768, 3072], P(None, 'tensor')
- grad_b_fc: float32 [3072], P('tensor')
- grad_w_proj: float32 [3072, 768], P('tensor')
- grad_b_proj: float32 [768], replicated
Inputs may be any that keep to these rules, and one draw needn't show every extreme that they name: `seq_lengths`: each row is either (1024, 1024) for two sequences or (2048, 0) for one; both kinds occur in every draw.
All inputs are finite; a program needn't handle non-finite values.
Results may differ from a plain program's by a relative error of at most 0.02.
Values may be sent and summed in bfloat16 or wider, within the bound.
A program may use at most 192 MiB of HBM per device.

v0:
```python
import jax
import jax.numpy as jnp
from jax import lax
from jax.sharding import PartitionSpec as P

SPAN = 64


NORM_EPS = 1e-05
PRECISE = lax.Precision.HIGHEST


def layer_norm(inputs, scale_vec, shift_vec):
    average = jnp.mean(inputs, axis=-1, keepdims=True)
    centred = inputs - average
    variance = jnp.mean(centred * centred, axis=-1, keepdims=True)
    return centred * lax.rsqrt(variance + NORM_EPS) * scale_vec + shift_vec


def feature(logits):
    return jnp.concatenate(
        [jax.nn.softmax(logits, axis=-1), jax.nn.softmax(-logits, axis=-1)], axis=-1
    )


def gelu_tanh(inputs):
    return jax.nn.gelu(inputs, approximate=True)


def span_links(lengths, span_count):
    first_end = lengths[0]
    second_end = lengths[0] + lengths[1]
    positions = jnp.arange(span_count, dtype=jnp.int32)
    starts = positions * SPAN
    seq_id = (starts >= first_end).astype(jnp.int32) + (starts >= second_end).astype(jnp.int32)
    linked = (positions[None, :] < positions[:, None]) & (seq_id[None, :] == seq_id[:, None])
    return linked.astype(jnp.float32)


def attention_forward(qkv_low, feat_q, feat_k, linked_mask):
    span_count = qkv_low.shape[0] // SPAN
    heads_here = feat_q.shape[0]
    head_size = feat_q.shape[1]
    blocks = qkv_low.reshape(span_count, SPAN, 3, heads_here, head_size)
    query_rows = blocks[:, :, 0]
    key_rows = blocks[:, :, 1]
    value_rows = blocks[:, :, 2]
    query_logits = jnp.einsum(
        "ncha,hab->nchb", query_rows, feat_q, preferred_element_type=jnp.float32
    )
    key_logits = jnp.einsum("ncha,hab->nchb", key_rows, feat_k, preferred_element_type=jnp.float32)
    query_feat = feature(query_logits).astype(jnp.bfloat16)
    key_feat = feature(key_logits).astype(jnp.bfloat16)
    causal = jnp.tril(jnp.ones((SPAN, SPAN), jnp.float32))
    scores = (
        jnp.einsum("nihf,njhf->nhij", query_feat, key_feat, preferred_element_type=jnp.float32)
        * causal
    )
    key_value = jnp.einsum(
        "njhf,njhe->nhfe", key_feat, value_rows, preferred_element_type=jnp.float32
    )
    key_total = jnp.sum(key_feat, axis=1, dtype=jnp.float32)
    carried = jnp.einsum("nm,mhfe->nhfe", linked_mask, key_value, precision=PRECISE)
    key_accum = jnp.einsum("nm,mhf->nhf", linked_mask, key_total, precision=PRECISE)
    carried_low = carried.astype(jnp.bfloat16)
    scores_low = scores.astype(jnp.bfloat16)
    numerator = jnp.einsum(
        "nhij,njhe->nihe", scores_low, value_rows, preferred_element_type=jnp.float32
    ) + jnp.einsum("nihf,nhfe->nihe", query_feat, carried_low, preferred_element_type=jnp.float32)
    denominator = jnp.transpose(jnp.sum(scores, axis=-1), (0, 2, 1)) + jnp.einsum(
        "nihf,nhf->nih", query_feat.astype(jnp.float32), key_accum, precision=PRECISE
    )
    return (
        query_rows,
        key_rows,
        value_rows,
        query_logits,
        key_logits,
        query_feat,
        key_feat,
        scores_low,
        carried_low,
        key_accum,
        numerator,
        denominator,
    )


def attention_backward(forward_parts, grad_mix, feat_q, feat_k, linked_mask):
    (
        query_rows,
        key_rows,
        value_rows,
        query_logits,
        key_logits,
        query_feat,
        key_feat,
        scores_low,
        carried_low,
        key_accum,
        numerator,
        denominator,
    ) = forward_parts
    total_rows = grad_mix.shape[0]
    grad_out = grad_mix.reshape(numerator.shape).astype(jnp.float32)
    mixing_full = numerator / denominator[..., None]
    grad_num = (grad_out / denominator[..., None]).astype(jnp.bfloat16)
    grad_den = -jnp.sum(grad_out * mixing_full, axis=-1) / denominator
    causal = jnp.tril(jnp.ones((SPAN, SPAN), jnp.float32))
    grad_scores = (
        jnp.einsum("nihe,njhe->nhij", grad_num, value_rows, preferred_element_type=jnp.float32)
        + jnp.transpose(grad_den, (0, 2, 1))[..., None]
    )
    grad_scores = (grad_scores * causal).astype(jnp.bfloat16)
    grad_carried = jnp.einsum(
        "nihf,nihe->nhfe", query_feat, grad_num, preferred_element_type=jnp.float32
    ).astype(jnp.bfloat16)
    grad_accum = jnp.einsum(
        "nihf,nih->nhf", query_feat.astype(jnp.float32), grad_den, precision=PRECISE
    )
    grad_kv = jnp.einsum(
        "nm,nhfe->mhfe", linked_mask, grad_carried.astype(jnp.float32), precision=PRECISE
    ).astype(jnp.bfloat16)
    grad_total = jnp.einsum("nm,nhf->mhf", linked_mask, grad_accum, precision=PRECISE)
    grad_qfeat = (
        jnp.einsum("nhij,njhf->nihf", grad_scores, key_feat, preferred_element_type=jnp.float32)
        + jnp.einsum("nihe,nhfe->nihf", grad_num, carried_low, preferred_element_type=jnp.float32)
        + grad_den[..., None] * key_accum[:, None]
    )
    grad_kfeat = (
        jnp.einsum("nhij,nihf->njhf", grad_scores, query_feat, preferred_element_type=jnp.float32)
        + jnp.einsum("nhfe,njhe->njhf", grad_kv, value_rows, preferred_element_type=jnp.float32)
        + grad_total[:, None]
    )
    grad_value = jnp.einsum(
        "nhij,nihe->njhe", scores_low, grad_num, preferred_element_type=jnp.float32
    ) + jnp.einsum("nhfe,njhf->njhe", grad_kv, key_feat, preferred_element_type=jnp.float32)
    grad_qlog = jax.vjp(feature, query_logits)[1](grad_qfeat)[0].astype(jnp.bfloat16)
    grad_klog = jax.vjp(feature, key_logits)[1](grad_kfeat)[0].astype(jnp.bfloat16)
    grad_query = jnp.einsum("nchb,hab->ncha", grad_qlog, feat_q, preferred_element_type=jnp.float32)
    grad_key = jnp.einsum("nchb,hab->ncha", grad_klog, feat_k, preferred_element_type=jnp.float32)
    grad_fq = jnp.einsum(
        "ncha,nchb->hab", query_rows, grad_qlog, preferred_element_type=jnp.float32
    )
    grad_fk = jnp.einsum("ncha,nchb->hab", key_rows, grad_klog, preferred_element_type=jnp.float32)
    grad_qkv = (
        jnp.stack([grad_query, grad_key, grad_value], axis=2)
        .reshape(total_rows, 3, -1)
        .astype(jnp.bfloat16)
    )
    return (grad_qkv, grad_fq, grad_fk)


def local(
    tokens_in,
    ln1_gain,
    ln1_bias,
    w_qkv,
    b_qkv,
    feat_q,
    feat_k,
    w_out,
    b_out,
    ln2_gain,
    ln2_bias,
    w_fc,
    b_fc,
    w_proj,
    b_proj,
    seq_lengths,
    cotangent,
):
    residual = tokens_in.astype(jnp.float32)
    normed_one = layer_norm(residual, ln1_gain, ln1_bias).astype(jnp.bfloat16)
    gathered_one = lax.all_gather(normed_one, "tensor", axis=0, tiled=True)
    qkv_low = (
        jnp.einsum("rd,dcw->rcw", gathered_one, w_qkv, preferred_element_type=jnp.float32) + b_qkv
    ).astype(jnp.bfloat16)
    span_count = qkv_low.shape[0] // SPAN
    linked_mask = span_links(seq_lengths[0], span_count)
    forward_parts = attention_forward(qkv_low, feat_q, feat_k, linked_mask)
    numerator = forward_parts[10]
    denominator = forward_parts[11]
    mixing = (numerator / denominator[..., None]).astype(jnp.bfloat16).reshape(qkv_low.shape[0], -1)
    attn_sum = lax.psum_scatter(
        jnp.dot(mixing, w_out, preferred_element_type=jnp.float32).astype(jnp.bfloat16),
        "tensor",
        scatter_dimension=0,
        tiled=True,
    ).astype(jnp.float32)
    mid_res = residual + attn_sum + b_out
    normed_two = layer_norm(mid_res, ln2_gain, ln2_bias).astype(jnp.bfloat16)
    gathered_two = lax.all_gather(normed_two, "tensor", axis=0, tiled=True)
    pre_act = jnp.dot(gathered_two, w_fc, preferred_element_type=jnp.float32) + b_fc
    act_low = gelu_tanh(pre_act).astype(jnp.bfloat16)
    unit_sum = lax.psum_scatter(
        jnp.dot(act_low, w_proj, preferred_element_type=jnp.float32).astype(jnp.bfloat16),
        "tensor",
        scatter_dimension=0,
        tiled=True,
    ).astype(jnp.float32)
    result = (mid_res + unit_sum + b_proj).astype(jnp.bfloat16)
    grad_res = cotangent.astype(jnp.float32)
    grad_b_proj = jnp.sum(grad_res, axis=0)
    grad_out_all = lax.all_gather(cotangent, "tensor", axis=0, tiled=True)
    grad_w_proj = jnp.einsum("rf,rd->fd", act_low, grad_out_all, preferred_element_type=jnp.float32)
    grad_act = jnp.einsum("rd,fd->rf", grad_out_all, w_proj, preferred_element_type=jnp.float32)
    grad_pre = jax.vjp(gelu_tanh, pre_act)[1](grad_act)[0].astype(jnp.bfloat16)
    grad_w_fc = jnp.einsum("rd,rf->df", gathered_two, grad_pre, preferred_element_type=jnp.float32)
    grad_b_fc = jnp.sum(grad_pre, axis=0, dtype=jnp.float32)
    grad_norm_two = lax.psum_scatter(
        jnp.einsum("rf,df->rd", grad_pre, w_fc, preferred_element_type=jnp.float32).astype(
            jnp.bfloat16
        ),
        "tensor",
        scatter_dimension=0,
        tiled=True,
    ).astype(jnp.float32)
    ln_two_back = jax.vjp(layer_norm, mid_res, ln2_gain, ln2_bias)[1]
    grad_mid, grad_ln2_gain, grad_ln2_bias = ln_two_back(grad_norm_two)
    grad_mid = grad_mid + grad_res
    grad_mid_low = grad_mid.astype(jnp.bfloat16)
    grad_b_out = jnp.sum(grad_mid_low, axis=0, dtype=jnp.float32)
    grad_head_all = lax.all_gather(grad_mid_low, "tensor", axis=0, tiled=True)
    grad_w_out = jnp.einsum("rw,rd->wd", mixing, grad_head_all, preferred_element_type=jnp.float32)
    grad_mix = jnp.einsum(
        "rd,wd->rw", grad_head_all, w_out, preferred_element_type=jnp.float32
    ).astype(jnp.bfloat16)
    grad_qkv, grad_feat_q, grad_feat_k = attention_backward(
        forward_parts, grad_mix, feat_q, feat_k, linked_mask
    )
    grad_w_qkv = jnp.einsum(
        "rd,rcw->dcw", gathered_one, grad_qkv, preferred_element_type=jnp.float32
    )
    grad_b_qkv = jnp.sum(grad_qkv, axis=0, dtype=jnp.float32)
    grad_norm_one = lax.psum_scatter(
        jnp.einsum("rcw,dcw->rd", grad_qkv, w_qkv, preferred_element_type=jnp.float32).astype(
            jnp.bfloat16
        ),
        "tensor",
        scatter_dimension=0,
        tiled=True,
    ).astype(jnp.float32)
    ln_one_back = jax.vjp(layer_norm, residual, ln1_gain, ln1_bias)[1]
    grad_first, grad_ln1_gain, grad_ln1_bias = ln_one_back(grad_norm_one)
    grad_input = (grad_first + grad_mid).astype(jnp.bfloat16)
    (
        grad_w_qkv,
        grad_b_qkv,
        grad_feat_q,
        grad_feat_k,
        grad_w_out,
        grad_w_fc,
        grad_b_fc,
        grad_w_proj,
    ) = lax.psum(
        (
            grad_w_qkv,
            grad_b_qkv,
            grad_feat_q,
            grad_feat_k,
            grad_w_out,
            grad_w_fc,
            grad_b_fc,
            grad_w_proj,
        ),
        "dp",
    )
    grad_ln1_gain, grad_ln1_bias, grad_b_out, grad_ln2_gain, grad_ln2_bias, grad_b_proj = lax.psum(
        (grad_ln1_gain, grad_ln1_bias, grad_b_out, grad_ln2_gain, grad_ln2_bias, grad_b_proj),
        ("dp", "tensor"),
    )
    return (
        result,
        grad_input,
        grad_ln1_gain,
        grad_ln1_bias,
        grad_w_qkv,
        grad_b_qkv,
        grad_feat_q,
        grad_feat_k,
        grad_w_out,
        grad_b_out,
        grad_ln2_gain,
        grad_ln2_bias,
        grad_w_fc,
        grad_b_fc,
        grad_w_proj,
        grad_b_proj,
    )


def solution(mesh):
    return jax.shard_map(
        local,
        mesh=mesh,
        in_specs=(
            P(("dp", "tensor"), None),
            P(),
            P(),
            P(None, None, "tensor"),
            P(None, "tensor"),
            P("tensor", None, None),
            P("tensor", None, None),
            P("tensor", None),
            P(),
            P(),
            P(),
            P(None, "tensor"),
            P("tensor"),
            P("tensor", None),
            P(),
            P("dp", None),
            P(("dp", "tensor"), None),
        ),
        out_specs=(
            P(("dp", "tensor"), None),
            P(("dp", "tensor"), None),
            P(),
            P(),
            P(None, None, "tensor"),
            P(None, "tensor"),
            P("tensor", None, None),
            P("tensor", None, None),
            P("tensor", None),
            P(),
            P(),
            P(),
            P(None, "tensor"),
            P("tensor"),
            P("tensor", None),
            P(),
        ),
        check_vma=False,
    )
```

profile of v0, /device:TPU:1, one launch (start us, length us, event | category | flops | bytes accessed | tf_op | source)
XLA Modules:
  0.0 914.0 jit_solution(1563867829012839398)
XLA Ops:
  16.0 62.3 %all-gather.5.cloned.1.call-done = bf16[2048,768]{1,0:T(8,128)(2,1)} async-done(((bf16[512,768]{1,0:T(8,128)(2,1)}), bf16[2048,768]{1,0:T(8,128)(2,1)}) %all-gather.5.cloned.1.call-update) | async-done | bytes 3145744 | tf_op jit(solution)/shard_map/all_gather | solution.py:175
  78.3 3.9 fusion.123
  83.9 8.0 reshape.202
  91.9 5.8 slice_bitcast_fusion
  111.9 16.8 %fusion.120 = (f32[32,64,3]{1,0,2:T(8,128)S(1)}, f32[32,64,3,64]{3,1,0,2:T(8,128)S(1)}) fusion(f32[3,32,64,64]{3,2,1,0:T(8,128)S(1)} %fusion.55), kind=kOutput, calls=%fused_computation.191 | output fusion | flops 1572927 | bytes 3170304 | tf_op jit(solution)/shard_map/sub | solution.py:22
  128.8 16.7 %fusion.121 = (f32[32,64,3]{1,0,2:T(8,128)S(1)}, f32[32,64,3,64]{3,1,0,2:T(8,128)S(1)}) fusion(f32[3,32,64,64]{3,2,1,0:T(8,128)S(1)} %fusion.55), kind=kOutput, calls=%fused_computation.192 | output fusion | flops 786495 | bytes 3170304 | tf_op jit(solution)/shard_map/sub | solution.py:22
  171.5 3.9 convolution_convert_fusion.2
  175.4 58.9 %reduce-scatter.5.cloned.1.call-done = bf16[512,768]{1,0:T(8,128)(2,1)} async-done(((bf16[2048,768]{1,0:T(8,128)(2,1)}), bf16[512,768]{1,0:T(8,128)(2,1)}) %reduce-scatter.5.cloned.1.call-update) | async-done | bytes 786448 | tf_op jit(solution)/shard_map/reduce_scatter | solution.py:185
  240.4 62.9 %all-gather.7.cloned.1.call-done = bf16[2048,768]{1,0:T(8,128)(2,1)} async-done(((bf16[512,768]{1,0:T(8,128)(2,1)}), bf16[2048,768]{1,0:T(8,128)(2,1)}) %all-gather.7.cloned.1.call-update) | async-done | bytes 3145744 | tf_op jit(solution)/shard_map/all_gather | solution.py:193
  303.3 7.5 fusion.124
  310.8 56.0 %all-gather.9.cloned.1.call-done = bf16[2048,768]{1,0:T(8,128)(2,1)} async-done(((bf16[512,768]{1,0:T(8,128)(2,1)}), bf16[2048,768]{1,0:T(8,128)(2,1)}) %all-gather.9.cloned.1.call-update) | async-done | bytes 3145744 | tf_op jit(solution)/shard_map/all_gather | solution.py:205
  366.9 12.6 %convert_reduce_fusion = (f32[768]{0:T(1024)}, bf16[2048,768]{1,0:T(8,128)(2,1)S(1)}, bf16[2048,768]{1,0:T(8,128)(2,1)}) fusion(f32[2048,768]{1,0:T(8,128)} %fusion.124, f32[768]{0:T(1024)} %param.29, bf16[2048,768]{1,0:T(8,128)(2,1)} %all-gather.9.cloned.1.call-done, bf16[768,768]{1,0:T(8,128)(2,1)S(1)} %copy-done), kind=kOutput, calls=%fused_computation.14 | convolution fusion | flops 2455239936 | bytes 16914432 | tf_op jit(solution)/shard_map/rd,fd->rf/dot_general | solution.py:207
  381.1 4.1 convolution_convert_fusion
  385.2 6.1 convolution_convert_fusion.1
  391.4 52.7 %reduce-scatter.9.cloned.1.call-done = bf16[512,768]{1,0:T(8,128)(2,1)} async-done(((bf16[2048,768]{1,0:T(8,128)(2,1)}), bf16[512,768]{1,0:T(8,128)(2,1)}) %reduce-scatter.9.cloned.1.call-update) | async-done | bytes 786448 | tf_op jit(solution)/shard_map/reduce_scatter | solution.py:211
  446.7 59.9 %reduce-scatter.7.cloned.1.call-done = bf16[512,768]{1,0:T(8,128)(2,1)} async-done(((bf16[2048,768]{1,0:T(8,128)(2,1)}), bf16[512,768]{1,0:T(8,128)(2,1)}) %reduce-scatter.7.cloned.1.call-update) | async-done | bytes 786448 | tf_op jit(solution)/shard_map/reduce_scatter | solution.py:196
  513.1 61.9 %all-gather.11.cloned.1.call-done = bf16[2048,768]{1,0:T(8,128)(2,1)} async-done(((bf16[512,768]{1,0:T(8,128)(2,1)}), bf16[2048,768]{1,0:T(8,128)(2,1)}) %all-gather.11.cloned.1.call-update) | async-done | bytes 3145744 | tf_op jit(solution)/shard_map/all_gather | solution.py:224
  575.0 4.2 fusion.21
  582.9 5.4 multiply_reduce_fusion.4
  607.4 4.1 bitcast_add_fusion.2
  611.7 4.6 multiply_reduce_fusion.3
  619.2 4.6 multiply_reduce_fusion.1
  623.8 4.8 add_convert_fusion.1
  637.0 8.8 add_convert_fusion.2
  658.3 4.1 bitcast_convert_fusion
  662.7 7.0 fusion.127
  669.7 4.2 fusion.126
  678.7 5.9 fusion.128
  686.3 35.0 %reduce-scatter.11.cloned.1.call-done = bf16[512,768]{1,0:T(8,128)(2,1)} async-done(((bf16[2048,768]{1,0:T(8,128)(2,1)}), bf16[512,768]{1,0:T(8,128)(2,1)}) %reduce-scatter.11.cloned.1.call-update) | async-done | bytes 786448 | tf_op jit(solution)/shard_map/reduce_scatter | solution.py:236
  727.1 40.8 %all-reduce = (f32[768]{0:T(1024)}, f32[768]{0:T(1024)}, f32[768]{0:T(1024)}, f32[768]{0:T(1024)}, f32[768]{0:T(1024)}, /*index=5*/f32[768]{0:T(1024)}) all-reduce(f32[768]{0:T(1024)S(1)} %get-tuple-element.22, f32[768]{0:T(1024)S(1)} %get-tuple-element.25, ...), channel_id=1, replica_groups=mesh['dp'=8,'tensor'=4] {'dp','tensor'}, use_global_device_ids=true, to_apply=%region_28.29 | all-reduce | flops 4608 | bytes 36864 | tf_op jit(solution)/shard_map/psum | solution.py:269
  767.9 12.3 %all-reduce.6.cloned.1.call-done = (f32[3,192]{1,0:T(4,128)}, f32[3,64,64]{2,1,0:T(8,128)}, f32[3,64,64]{2,1,0:T(8,128)}, f32[768]{0:T(1024)}) async-done(((f32[3,192]{1,0:T(4,128)}, f32[3,64,64]{2,1,0:T(8,128)}, f32[3,64,64]{2,1,0:T(8,128)}, f32[768]{0:T(1024)}), (f32[3,192]{1,0:T(4,128)}, f32[3,64,64]{2,1,0:T(8,128)}, f32[3,64,64]{2,1,0:T(8,128)}, f32[768]{0:T(1024)})) %all-reduce.6.cloned.1.call-update) | async-done | bytes 103696 | tf_op jit(solution)/shard_map/psum | solution.py:256
  780.2 117.2 %all-reduce.8.cloned.1.call-done = (f32[768,3,192]{0,2,1:T(8,128)}, f32[192,768]{1,0:T(8,128)}, f32[768,768]{1,0:T(8,128)}, f32[768,768]{1,0:T(8,128)}) async-done(((f32[768,3,192]{0,2,1:T(8,128)}, f32[192,768]{1,0:T(8,128)}, f32[768,768]{1,0:T(8,128)}, f32[768,768]{1,0:T(8,128)}), (f32[768,3,192]{0,2,1:T(8,128)}, f32[192,768]{1,0:T(8,128)}, f32[768,768]{1,0:T(8,128)}, ...) | async-done | bytes 7077904 | tf_op jit(solution)/shard_map/psum | solution.py:256
  (311 shorter events, 134.2 us)
Async XLA Ops:
  7.2 359.7 %copy-start = (bf16[768,768]{1,0:T(8,128)(2,1)S(1)}, bf16[768,768]{1,0:T(8,128)(2,1)}, u32[]{:S(2)}) copy-start(bf16[768,768]{1,0:T(8,128)(2,1)} %param.30) | copy-start | bytes 3538948
  7.2 71.0 %all-gather.5.cloned.1.call-start = ((), (), s32[]{:S(2)}) async-start(), calls=%async_computation.4 | async-start | bytes 3932160 | tf_op jit(solution)/shard_map/all_gather | solution.py:175
  8.7 69.5 %copy-start.98 = (bf16[768,3,192]{0,2,1:T(8,128)(2,1)S(1)}, bf16[768,3,192]{0,2,1:T(8,128)(2,1)}, u32[]{:S(2)}) copy-start(bf16[768,3,192]{0,2,1:T(8,128)(2,1)} %param.20) | copy-start | bytes 2654212
  12.8 221.6 %reduce-scatter.5.cloned.1.call-start = ((), (), s32[]{:S(2)}) async-start(), calls=%async_computation.5 | async-start | bytes 3932160 | tf_op jit(solution)/shard_map/reduce_scatter | solution.py:185
  111.9 33.6 %copy-start.53 = (f32[32,64,3]{1,0,2:T(8,128)S(1)}, f32[32,64,3]{1,0,2:T(8,128)}, u32[]{:S(2)}) copy-start(f32[32,64,3]{1,0,2:T(8,128)} %get-tuple-element.63) | copy-start | bytes 73732
  128.7 25.6 %copy-start.4 = (f32[32,64,3,64]{3,1,0,2:T(8,128)}, f32[32,64,3,64]{3,1,0,2:T(8,128)S(1)}, u32[]{:S(2)}) copy-start(f32[32,64,3,64]{3,1,0,2:T(8,128)S(1)} %get-tuple-element.66) | copy-start | bytes 4718596
  128.7 25.6 %copy-start.47 = (f32[32,64,3]{1,0,2:T(8,128)}, f32[32,64,3]{1,0,2:T(8,128)S(1)}, u32[]{:S(2)}) copy-start(f32[32,64,3]{1,0,2:T(8,128)S(1)} %get-tuple-element.65) | copy-start | bytes 73732
  128.7 16.8 %copy-start.8 = (f32[32,64,3,64]{3,1,0,2:T(8,128)S(1)}, f32[32,64,3,64]{3,1,0,2:T(8,128)}, u32[]{:S(2)}) copy-start(f32[32,64,3,64]{3,1,0,2:T(8,128)} %get-tuple-element.62) | copy-start | bytes 4718596
  128.7 16.8 %copy-start.10 = (f32[32,64,3,64]{3,1,0,2:T(8,128)S(1)}, f32[32,64,3,64]{3,1,0,2:T(8,128)}, u32[]{:S(2)}) copy-start(f32[32,64,3,64]{3,1,0,2:T(8,128)} %get-tuple-element.64) | copy-start | bytes 4718596
  128.7 16.8 %copy-start.51 = (f32[32,64,3]{1,0,2:T(8,128)S(1)}, f32[32,64,3]{1,0,2:T(8,128)}, u32[]{:S(2)}) copy-start(f32[32,64,3]{1,0,2:T(8,128)} %get-tuple-element.61) | copy-start | bytes 73732
  175.4 59.0 %copy-start.72 = (f32[768]{0:T(1024)S(1)}, f32[768]{0:T(1024)}, u32[]{:S(2)}) copy-start(f32[768]{0:T(1024)} %param.25) | copy-start | bytes 9220
  175.4 62.1 %copy-start.79 = (f32[768]{0:T(1024)S(1)}, f32[768]{0:T(1024)}, u32[]{:S(2)}) copy-start(f32[768]{0:T(1024)} %param.26) | copy-start | bytes 9220
  175.4 127.9 %all-gather.7.cloned.1.call-start = ((), (), s32[]{:S(2)}) async-start(), calls=%async_computation.6 | async-start | bytes 3932160 | tf_op jit(solution)/shard_map/all_gather | solution.py:193
  239.6 127.3 %all-gather.9.cloned.1.call-start = ((), (), s32[]{:S(2)}) async-start(), calls=%async_computation.8 | async-start | bytes 3932160 | tf_op jit(solution)/shard_map/all_gather | solution.py:205
  240.2 204.0 %reduce-scatter.9.cloned.1.call-start = ((), (), s32[]{:S(2)}) async-start(), calls=%async_computation.9 | async-start | bytes 3932160 | tf_op jit(solution)/shard_map/reduce_scatter | solution.py:211
  366.9 14.2 %copy-start.97 = (bf16[768,768]{1,0:T(8,128)(2,1)S(1)}, bf16[768,768]{1,0:T(8,128)(2,1)}, u32[]{:S(2)}) copy-start(bf16[768,768]{1,0:T(8,128)(2,1)} %param.28) | copy-start | bytes 3538948
  385.2 121.5 %reduce-scatter.7.cloned.1.call-start = ((), (), s32[]{:S(2)}) async-start(), calls=%async_computation.7 | async-start | bytes 3932160 | tf_op jit(solution)/shard_map/reduce_scatter | solution.py:196
  391.3 52.8 %copy-start.20 = (bf16[512,768]{1,0:T(8,128)(2,1)S(1)}, bf16[512,768]{1,0:T(8,128)(2,1)}, u32[]{:S(2)}) copy-start(bf16[512,768]{1,0:T(8,128)(2,1)} %reduce-scatter.5.cloned.1.call-done) | copy-start | bytes 2359300
  391.3 52.8 %copy-start.83 = (f32[512]{0:T(512)S(1)}, f32[512]{0:T(512)}, u32[]{:S(2)}) copy-start(f32[512]{0:T(512)} %copy-done.82) | copy-start | bytes 6148
  391.4 55.3 %copy-start.87 = (f32[512]{0:T(512)S(1)}, f32[512]{0:T(512)}, u32[]{:S(2)}) copy-start(f32[512]{0:T(512)} %copy-done.86) | copy-start | bytes 6148
  391.4 115.3 %copy-start.92 = (f32[768]{0:T(1024)S(1)}, f32[768]{0:T(1024)}, u32[]{:S(2)}) copy-start(f32[768]{0:T(1024)} %param.31) | copy-start | bytes 9220
  391.4 183.6 %all-gather.11.cloned.1.call-start = ((), (), s32[]{:S(2)}) async-start(), calls=%async_computation.10 | async-start | bytes 3932160 | tf_op jit(solution)/shard_map/all_gather | solution.py:224
  509.9 65.1 %copy-start.46 = (bf16[192,768]{1,0:T(8,128)(2,1)S(1)}, bf16[192,768]{1,0:T(8,128)(2,1)}, u32[]{:S(2)}) copy-start(bf16[192,768]{1,0:T(8,128)(2,1)} %param.24) | copy-start | bytes 884740
  511.3 210.1 %reduce-scatter.11.cloned.1.call-start = ((), (), s32[]{:S(2)}) async-start(), calls=%async_computation.11 | async-start | bytes 3932160 | tf_op jit(solution)/shard_map/reduce_scatter | solution.py:236
  637.0 10.0 %copy-start.69 = (bf16[3,64,64]{2,1,0:T(8,128)(2,1)S(1)}, bf16[3,64,64]{2,1,0:T(8,128)(2,1)}, u32[]{:S(2)}) copy-start(bf16[3,64,64]{2,1,0:T(8,128)(2,1)} %param.22) | copy-start | bytes 73732
  662.4 117.7 %all-reduce.6.cloned.1.call-start = ((), (), s32[]{:S(2)}) async-start(), calls=%async_computation.12 | async-start | bytes 409600 | tf_op jit(solution)/shard_map/psum | solution.py:256
  678.6 218.7 %all-reduce.8.cloned.1.call-start = ((), (), s32[]{:S(2)}) async-start(), calls=%async_computation.13 | async-start | bytes 14155776 | tf_op jit(solution)/shard_map/psum | solution.py:256
  686.3 35.1 %copy-start.76 = (f32[512]{0:T(512)S(1)}, f32[512]{0:T(512)}, u32[]{:S(2)}) copy-start(f32[512]{0:T(512)} %copy-done.75) | copy-start | bytes 6148
  686.3 35.1 %copy-start.78 = (f32[768]{0:T(1024)S(1)}, f32[768]{0:T(1024)}, u32[]{:S(2)}) copy-start(f32[768]{0:T(1024)} %param.18) | copy-start | bytes 9220
  686.3 36.9 %copy-start.85 = (f32[512]{0:T(512)S(1)}, f32[512]{0:T(512)}, u32[]{:S(2)}) copy-start(f32[512]{0:T(512)} %copy-done.84) | copy-start | bytes 6148
  686.3 36.9 %copy-start.81 = (f32[512]{0:T(512)S(1)}, f32[512]{0:T(512)}, u32[]{:S(2)}) copy-start(f32[512]{0:T(512)} %copy-done.80) | copy-start | bytes 6148
  686.3 39.0 %copy-start.29 = (f32[512,768]{1,0:T(8,128)S(1)}, f32[512,768]{1,0:T(8,128)}, u32[]{:S(2)}) copy-start(f32[512,768]{1,0:T(8,128)} %copy-done.28) | copy-start | bytes 4718596
  (80 other events, 273.5 us)
Sparse Core Ops, SparseCore 0:
  12.9 65.3 all-gather.4
  175.5 58.7 reduce-scatter.4
  239.7 63.5 all-gather.6
  304.7 62.0 all-gather.8
  385.3 58.8 reduce-scatter.8
  446.3 60.2 reduce-scatter.6
  511.4 63.5 all-gather.10
  662.5 58.7 reduce-scatter.10
  726.0 54.1 all-reduce.5
  784.8 112.4 all-reduce.7
where the time goes:
time: 924 us; the launch traced here: 914 us
  waiting for transfers between devices  580 us (63%)
  matrix products  103 us (11%)
  other arithmetic  101 us (11%)
  local copies, waits for them, and re-layouts  71.2 us (8%)
  blocking collectives  40.8 us (4%)
  between operations  16.9 us (2%)
    psum x2, waiting for transfers between devices, local(): lax.psum((grad_w_qkv, grad_b_qkv, grad_feat_q, grad_feat_k, grad_w_out, g...  129 us
    all_gather x1, waiting for transfers between devices, local(): gathered_two = lax.all_gather(normed_two, 'tensor', axis=0, tiled=True)  62.9 us
    all_gather x1, waiting for transfers between devices, local(): gathered_one = lax.all_gather(normed_one, 'tensor', axis=0, tiled=True)  62.3 us
    all_gather x1, waiting for transfers between devices, local(): grad_head_all = lax.all_gather(grad_mid_low, 'tensor', axis=0, tiled=True)  61.9 us
    reduce_scatter x1, waiting for transfers between devices, local(): lax.psum_scatter(jnp.dot(act_low, w_proj, preferred_element_type=jnp.floa...  59.9 us
    reduce_scatter x1, waiting for transfers between devices, local(): lax.psum_scatter(jnp.dot(mixing, w_out, preferred_element_type=jnp.float3...  58.9 us
    all_gather x1, waiting for transfers between devices, local(): grad_out_all = lax.all_gather(cotangent, 'tensor', axis=0, tiled=True)  56 us
    reduce_scatter x1, waiting for transfers between devices, local(): lax.psum_scatter(jnp.einsum('rf,df->rd', grad_pre, w_fc, preferred_elemen...  52.7 us
  transfers between devices with their start and end apart: 10, of which 10 were waited for; matrix products, arithmetic and copies ran while one was open for 5% of the time, Pallas kernels for 0%

commit v1 on v0

v1 whole, which is shorter than its diff:
```python
import functools
import math

import jax
import jax.numpy as jnp
from jax import lax
from jax.experimental import pallas as pl
from jax.experimental.pallas import tpu as pltpu
from jax.sharding import PartitionSpec as P

NORM_EPS = 1e-05
BF = jnp.bfloat16
F32 = jnp.float32
MESH = pl.DeviceIdType.MESH
NT = 4
D = 768
HD = 64
HPG = 3
HC = HPG * HD
NH = NT * HPG
U = 768
AUG = 80
QKV = 3 * HC
KINDS = 3
R_W = 96
R_G = (112, 96, 96)
ROWS_G = (896, 768, 768)
CB = 256


def dot(a, b, ca=1, cb=0):
    return lax.dot_general(a, b, (((ca,), (cb,)), ((), ())), preferred_element_type=F32)


def mo(value, multiple):
    return pl.multiple_of(value, multiple)


def soft_pair(logits):
    top = jnp.max(logits, axis=0, keepdims=True)
    low = jnp.min(logits, axis=0, keepdims=True)
    e_pos = jnp.exp(logits - top)
    e_neg = jnp.exp(low - logits)
    p = e_pos * (1.0 / jnp.sum(e_pos, axis=0, keepdims=True))
    m = e_neg * (1.0 / jnp.sum(e_neg, axis=0, keepdims=True))
    return jnp.concatenate([p, m], axis=0)


def norm_stats(rows):
    mean = jnp.mean(rows, axis=-1, keepdims=True)
    centred = rows - mean
    var = jnp.mean(centred * centred, axis=-1, keepdims=True)
    inv = lax.rsqrt(var + NORM_EPS)
    return centred * inv, inv


def col(n):
    return pl.ds(mo(n * CB, CB), CB)


def layer_kernel(
    nh,
    seq_ref,
    x_ref,
    cot_ref,
    ln1g_ref,
    ln1b_ref,
    bout_ref,
    ln2g_ref,
    ln2b_ref,
    bproj_ref,
    a_own,
    b_own,
    c_own,
    ft_own,
    bp_own,
    res_ref,
    gin_ref,
    oa_ref,
    ob_ref,
    oc_ref,
    ov_ref,
    WA,
    WB,
    WC,
    FT,
    BP,
    R0A,
    R0B,
    R0C,
    RAA,
    RAB,
    RAC,
    RBA,
    RBB,
    RBC,
    ZRA,
    ZRB,
    ZRC,
    OA,
    OB,
    OC,
    RHA,
    RHB,
    RHC,
    LS,
    LR,
    LZ,
    N1,
    QK,
    VA,
    QF,
    KF,
    NM,
    ST,
    CT,
    CR,
    SQ,
    GR,
    MX,
    DI,
    MID,
    N2,
    N2T,
    UN,
    GN2,
    GML,
    ACT,
    ACTT,
    GP,
    GBF,
    GA,
    GC,
    GQ,
    VS,
    own_s,
    sm_s,
    sm_r,
    wz_s,
    w_s,
    w_r,
    g_s,
    g_r,
    z_r,
    o_s,
    o_r,
    h_s,
    h_r,
    l_s,
    l_r,
    lz_s,
    lz_r,
    c_s,
    c_r,
):
    dp = lax.axis_index("dp")
    z = lax.axis_index("tensor")
    T = x_ref.shape[0]
    NB = T // CB
    core = lax.rem(dp, 2)
    bx = lax.rem(dp // 2, 2)
    by = lax.rem(dp // 4, 2)
    d_core = 1 - 2 * core
    d_x = 2 * (1 - 2 * bx)
    d_y = 4 * (1 - 2 * by)
    slot = core * 4 + by * 2 + bx

    W = (WA, WB, WC)
    OWN = (a_own, b_own, c_own)
    R0 = (R0A, R0B, R0C)
    RA = (RAA, RAB, RAC)
    RB = (RBA, RBB, RBC)
    ZR = (ZRA, ZRB, ZRC)
    O = (OA, OB, OC)
    RH = (RHA, RHB, RHC)

    def order(j):
        return jnp.where(j == 0, z, j - 1 + (j - 1 >= z).astype(jnp.int32))

    def high(i):
        step = 8 * 2**i
        return dp + step * (1 - 2 * lax.rem(dp // step, 2))

    def rcopy(src, dst, ssem, rsem, dev):
        return pltpu.make_async_remote_copy(
            src_ref=src, dst_ref=dst, send_sem=ssem, recv_sem=rsem, device_id=dev, device_id_type=MESH
        )

    def first_is_y(k, g):
        return lax.rem(k + g, 2)

    def step_a(k, g):
        q = first_is_y(k, g)
        return dp + q * d_y + (1 - q) * d_x

    def step_b(k, g):
        q = first_is_y(k, g)
        return dp + q * d_x + (1 - q) * d_y

    def slot_of(k, g, flip_a, flip_b):
        q = first_is_y(k, g)
        sx = bx + (1 - 2 * bx) * (q * flip_b + (1 - q) * flip_a)
        sy = by + (1 - 2 * by) * (q * flip_a + (1 - q) * flip_b)
        return core * 4 + sy * 2 + sx

    def abs_slot(k, g, flip_a, bit_b):
        q = first_is_y(k, g)
        ax = bx + (1 - 2 * bx) * flip_a
        ay = by + (1 - 2 * by) * flip_a
        sx = q * bit_b + (1 - q) * ax
        sy = q * ay + (1 - q) * bit_b
        return core * 4 + sy * 2 + sx

    def my_b_bit(k, g):
        q = first_is_y(k, g)
        return q * bx + (1 - q) * by

    peers = [(dp + d_core, z), (dp + d_x, z), (dp + d_y, z)]
    peers += [(high(i), z) for i in range(nh)]
    peers += [(dp, lax.rem(z + o, NT)) for o in range(1, NT)]
    barrier = pltpu.get_barrier_semaphore()
    for peer in peers:
        pl.semaphore_signal(barrier, inc=1, device_id=peer, device_id_type=MESH)
    pl.semaphore_wait(barrier, len(peers))

    def wrows(k, g, s):
        return W[k].at[g, pl.ds(mo(s * R_W, R_W), R_W), :]

    def wrows4(k, g, c):
        return W[k].at[g, pl.ds(mo(c * 4 * R_W, R_W), 4 * R_W), :]

    def w_z(k):
        for o in range(1, NT):
            rcopy(
                OWN[k].at[pl.ds(mo(slot * R_W, R_W), R_W), :],
                wrows(k, z, slot),
                wz_s.at[k, o - 1],
                w_r.at[0, k, z],
                (dp, lax.rem(z + o, NT)),
            ).start()

    def w_wait(k, g, stage, ref):
        rcopy(ref, ref, w_s.at[0, k, g], w_r.at[stage, k, g], (dp + d_core, z)).wait_recv()

    def w_1(k, i):
        g = order(i)
        w_wait(k, g, 0, wrows(k, g, slot))
        src = wrows(k, g, slot)
        rcopy(src, src, w_s.at[0, k, g], w_r.at[1, k, g], (step_a(k, g), z)).start()

    def w_2(k, i):
        g = order(i)
        w_wait(k, g, 1, wrows(k, g, slot_of(k, g, 1, 0)))
        for f in range(2):
            src = wrows(k, g, slot_of(k, g, f, 0))
            rcopy(src, src, w_s.at[1 + f, k, g], w_r.at[2 + f, k, g], (step_b(k, g), z)).start()

    def w_3(k, i):
        g = order(i)
        for f in range(2):
            w_wait(k, g, 2 + f, wrows(k, g, slot_of(k, g, f, 1)))
        src = wrows4(k, g, core)
        rcopy(src, src, w_s.at[3, k, g], w_r.at[4, k, g], (dp + d_core, z)).start()

    def w_4(k, i):
        g = order(i)
        w_wait(k, g, 4, wrows4(k, g, 1 - core))
        one = wrows(k, g, slot)
        for st in range(3):
            rcopy(one, one, w_s.at[st, k, g], w_r.at[0, k, g], (dp + d_core, z)).wait_send()
        four = wrows4(k, g, core)
        rcopy(four, four, w_s.at[3, k, g], w_r.at[0, k, g], (dp + d_core, z)).wait_send()

    def w_z_done(k):
        one = OWN[k].at[pl.ds(mo(slot * R_W, R_W), R_W), :]
        for o in range(1, NT):
            rcopy(one, one, wz_s.at[k, o - 1], w_r.at[0, k, z], (dp, lax.rem(z + o, NT))).wait_send()

    small = ((ft_own, FT), (bp_own, BP))

    def small_send():
        for i, (own, buf) in enumerate(small):
            for o in range(1, NT):
                rcopy(own, buf.at[z], sm_s.at[i, o - 1], sm_r.at[i, z], (dp, lax.rem(z + o, NT))).start()

    def small_wait(g):
        for i, (own, buf) in enumerate(small):
            rcopy(own, buf.at[g], sm_s.at[i, 0], sm_r.at[i, g], (dp, z)).wait_recv()

    def small_done():
        for i, (own, buf) in enumerate(small):
            for o in range(1, NT):
                rcopy(own, buf.at[z], sm_s.at[i, o - 1], sm_r.at[i, z], (dp, lax.rem(z + o, NT))).wait_send()

    local = [
        pltpu.make_async_copy(ft_own, FT.at[z], own_s.at[0]),
        pltpu.make_async_copy(bp_own, BP.at[z], own_s.at[1]),
        pltpu.make_async_copy(a_own, WA.at[z, pl.ds(0, D), :], own_s.at[2]),
        pltpu.make_async_copy(b_own, WB.at[z], own_s.at[3]),
        pltpu.make_async_copy(c_own, WC.at[z], own_s.at[4]),
    ]
    small_send()
    w_z(0)
    for copy in local:
        copy.start()

    def grows(k, g, s, n=1):
        return W[k].at[g, pl.ds(mo(s * R_G[k], 16), n * R_G[k]), :]

    def add_rows(dst, start, src, n):
        blk = 16 if n % 32 else 32

        def body(i, _):
            at = pl.ds(mo(start + i * blk, 16), blk)
            dst[at, :] = (dst[at, :].astype(F32) + src[pl.ds(mo(i * blk, 16), blk), :].astype(F32)).astype(BF)
            return 0

        lax.fori_loop(0, n // blk, body, 0)

    def g_wait(k, g, stage, ref):
        rcopy(ref, ref, g_s.at[0, k, g], g_r.at[stage, k, g], (dp + d_core, z)).wait_recv()

    def g_core(k, g):
        rcopy(
            grows(k, g, (1 - core) * 4, 4), R0[k].at[g], g_s.at[0, k, g], g_r.at[0, k, g], (dp + d_core, z)
        ).start()

    def g_a(k, g):
        g_wait(k, g, 0, R0[k].at[g])
        add_rows(W[k].at[g], core * 4 * R_G[k], R0[k].at[g], 4 * R_G[k])
        for b in range(2):
            rcopy(
                grows(k, g, abs_slot(k, g, 1, b)),
                RA[k].at[g, b],
                g_s.at[1 + b, k, g],
                g_r.at[1 + b, k, g],
                (step_a(k, g), z),
            ).start()

    def g_b(k, g):
        for b in range(2):
            g_wait(k, g, 1 + b, RA[k].at[g, b])
            add_rows(W[k].at[g], abs_slot(k, g, 0, b) * R_G[k], RA[k].at[g, b], R_G[k])
        rcopy(
            grows(k, g, slot_of(k, g, 0, 1)),
            RB[k].at[g],
            g_s.at[3, k, g],
            g_r.at[3, k, g],
            (step_b(k, g), z),
        ).start()

    def g_z(k, g):
        g_wait(k, g, 3, RB[k].at[g])
        add_rows(W[k].at[g], slot * R_G[k], RB[k].at[g], R_G[k])

        @pl.when(g != z)
        def _():
            rcopy(grows(k, g, slot), ZR[k].at[z], g_s.at[4, k, g], z_r.at[k, z], (dp, g)).start()

    def g_done(k, g):
        four = grows(k, g, 0, 4)
        one = grows(k, g, 0)
        rcopy(four, four, g_s.at[0, k, g], g_r.at[0, k, g], (dp + d_core, z)).wait_send()
        for st in range(1, 4):
            rcopy(one, one, g_s.at[st, k, g], g_r.at[0, k, g], (dp + d_core, z)).wait_send()

        @pl.when(g != z)
        def _():
            rcopy(one, one, g_s.at[4, k, g], g_r.at[0, k, g], (dp + d_core, z)).wait_send()

    def orows(k, s, n=1):
        return O[k].at[pl.ds(mo(s * R_G[k], 16), n * R_G[k]), :]

    def o_wait(k, stage, ref):
        rcopy(ref, ref, o_s.at[stage, k], o_r.at[stage, k], (dp + d_core, z)).wait_recv()

    def g_sum(k):
        for o in range(1, NT):
            zz = lax.rem(z + o, NT)
            ref = ZR[k].at[zz]
            rcopy(ref, ref, g_s.at[0, k, 0], z_r.at[k, zz], (dp, z)).wait_recv()
        blk = 16

        def body(i, _):
            at = pl.ds(mo(i * blk, 16), blk)
            mine = pl.ds(mo(slot * R_G[k] + i * blk, 16), blk)
            acc = W[k][z, mine, :].astype(F32)
            for o in range(1, NT):
                acc = acc + ZR[k][lax.rem(z + o, NT), at, :].astype(F32)
            O[k][mine, :] = acc.astype(BF)
            return 0

        lax.fori_loop(0, R_G[k] // blk, body, 0)
        for i in range(nh):
            rcopy(orows(k, slot), RH[k].at[i], h_s.at[i, k], h_r.at[i, k], (high(i), z)).start()
            rcopy(orows(k, slot), RH[k].at[i], h_s.at[i, k], h_r.at[i, k], (high(i), z)).wait()
            add_rows(O[k], slot * R_G[k], RH[k].at[i], R_G[k])
        src = orows(k, slot)
        rcopy(src, src, o_s.at[0, k], o_r.at[0, k], (step_b(k, z), z)).start()

    def o_2(k):
        o_wait(k, 0, orows(k, slot_of(k, z, 0, 1)))
        for f in range(2):
            src = orows(k, slot_of(k, z, 0, f))
            rcopy(src, src, o_s.at[1 + f, k], o_r.at[1 + f, k], (step_a(k, z), z)).start()

    def o_3(k):
        for f in range(2):
            o_wait(k, 1 + f, orows(k, slot_of(k, z, 1, f)))
        src = orows(k, core * 4, 4)
        rcopy(src, src, o_s.at[3, k], o_r.at[3, k], (dp + d_core, z)).start()

    def o_4(k, out, sem):
        o_wait(k, 3, orows(k, (1 - core) * 4, 4))
        copy = pltpu.make_async_copy(O[k], out, sem)
        copy.start()
        one = orows(k, slot)
        for st in range(3):
            rcopy(one, one, o_s.at[st, k], o_r.at[0, k], (dp + d_core, z)).wait_send()
        four = orows(k, core * 4, 4)
        rcopy(four, four, o_s.at[3, k], o_r.at[0, k], (dp + d_core, z)).wait_send()
        return copy

    def iota(shape, axis):
        return lax.broadcasted_iota(jnp.int32, shape, axis)

    causal = iota((CB, CB), 0) <= iota((CB, CB), 1)
    aug_tail = jnp.where(iota((16, T), 0) < 2, 1.0, 0.0).astype(BF)
    ones_rows = jnp.ones((16, T), BF)
    head_mask = (iota((HC, HC), 0) // HD) == (iota((HC, HC), 1) // HD)

    def pick(which):
        r = iota((2 * HD, HC), 0) - which * HD
        return (r == lax.rem(iota((2 * HD, HC), 1), HD)).astype(BF)

    def pick_back(which):
        r = iota((HC, 2 * HD), 1) - which * HD
        return (r == lax.rem(iota((HC, 2 * HD), 0), HD)).astype(BF)

    def block_diag(g, which):
        return jnp.where(head_mask, dot(FT[g], pick(which)), 0.0).astype(BF)

    first_end = seq_ref[0, 0]
    second_end = seq_ref[0, 0] + seq_ref[0, 1]

    def seq_id(zz):
        start = zz * T
        return (start >= first_end).astype(jnp.int32) + (start >= second_end).astype(jnp.int32)

    from_prev = jnp.logical_and(z > 0, seq_id(z) == seq_id(z - 1))
    from_next = jnp.logical_and(z < NT - 1, seq_id(z) == seq_id(z + 1))

    RB_ = 64

    def p0(i, _):
        at = pl.ds(mo(i * RB_, RB_), RB_)
        xh, _inv = norm_stats(x_ref[at, :].astype(F32))
        N1[at, :] = (xh * ln1g_ref[...] + ln1b_ref[...]).astype(BF)
        return 0

    lax.fori_loop(0, T // RB_, p0, 0)
    for g in range(NT):
        WA[g, pl.ds(D, ROWS_G[0] - D), :] = jnp.zeros((ROWS_G[0] - D, D), BF)
    GQ[pl.ds(QKV, D - QKV), :] = jnp.zeros((D - QKV, T), BF)

    @pl.when(z == 0)
    def _():
        CR[...] = jnp.zeros_like(CR)

    @pl.when(z == NT - 1)
    def _():
        GR[...] = jnp.zeros_like(GR)

    for copy in local[:3]:
        copy.wait()

    def p1(j, _):
        g = order(j)

        @pl.when(j == 1)
        def _():
            small_wait(order(1))
            w_1(0, 1)
            w_1(0, 2)
            w_2(0, 1)
            w_1(0, 3)
            w_z(1)
            w_2(0, 2)
            w_3(0, 1)
            w_2(0, 3)
            w_3(0, 2)
            w_4(0, 1)

        @pl.when(j == 2)
        def _():
            small_wait(order(2))
            w_3(0, 3)
            w_4(0, 2)

        @pl.when(j == 3)
        def _():
            small_wait(order(3))
            w_4(0, 3)
            w_1(1, 1)
            w_1(1, 2)
            w_1(1, 3)
            w_z(2)

        bias = jnp.transpose(BP[g])[:QKV, 0:1]
        qkv = (dot(WA[g, pl.ds(0, QKV), :], N1[...], 1, 1) + bias).astype(BF)
        QK[g] = qkv[: 2 * HC]
        ql = dot(block_diag(g, 0), qkv[:HC])
        kl = dot(block_diag(g, 1), qkv[HC : 2 * HC])
        for h in range(HPG):
            hh = g * HPG + h
            rows = slice(h * HD, (h + 1) * HD)
            qf = soft_pair(ql[rows]).astype(BF)
            kf = soft_pair(kl[rows]).astype(BF)
            va = jnp.concatenate([qkv[2 * HC + h * HD : 2 * HC + (h + 1) * HD], aug_tail], axis=0)
            QF[hh] = qf
            KF[hh] = kf
            VA[hh] = va
            kn = kf.T
            ST[hh] = dot(va, kn)
            for qi in range(NB):
                qs = slice(qi * CB, (qi + 1) * CB)
                acc = None
                for ki in range(qi + 1):
                    ks = slice(ki * CB, (ki + 1) * CB)
                    s = dot(kn[ks], qf[:, qs])
                    if ki == qi:
                        s = jnp.where(causal, s, 0.0)
                    part = dot(va[:, ks], s.astype(BF))
                    acc = part if acc is None else acc + part
                NM[hh, :, qs] = acc[: HD + 8]
        return 0

    lax.fori_loop(0, NT, p1, 0)
    w_2(1, 1)
    w_2(1, 2)
    w_2(1, 3)

    def chain_wait(buf, g, stage):
        rcopy(buf.at[g], buf.at[g], c_s.at[stage, g], c_r.at[stage, g], (dp, z)).wait_recv()

    def p1b(g, _):
        @pl.when(z > 0)
        def _():
            chain_wait(CR, g, 0)

        for h in range(HPG):
            hh = g * HPG + h
            carried = jnp.where(from_prev, CR[g, h].astype(F32), 0.0)
            SQ[g, h] = (ST[hh] + carried).astype(BF)
            CT[hh] = carried.astype(BF)

        @pl.when(z < NT - 1)
        def _():
            rcopy(SQ.at[g], CR.at[g], c_s.at[0, g], c_r.at[0, g], (dp, z + 1)).start()

        for h in range(HPG):
            hh = g * HPG + h
            num = NM[hh] + dot(CT[hh], QF[hh])[: HD + 8]
            inv = 1.0 / num[HD : HD + 1]
            DI[hh] = inv
            MX[g, pl.ds(h * HD, HD), :] = (num[:HD] * inv).astype(BF)
        return 0

    lax.fori_loop(0, NT, p1b, 0)
    w_3(1, 1)
    w_3(1, 2)
    w_3(1, 3)

    def p2(n, _):
        acc = None
        for g in range(NT):
            part = dot(MX[g], WA[g, pl.ds(QKV, HC), col(n)], 0, 0)
            acc = part if acc is None else acc + part
        MID[:, col(n)] = x_ref[:, col(n)].astype(F32) + (acc + bout_ref[:, col(n)])
        return 0

    lax.fori_loop(0, D // CB, p2, 0)

    def p2b(i, _):
        at = pl.ds(mo(i * 128, 128), 128)
        xh, _inv = norm_stats(MID[at, :])
        n2 = (xh * ln2g_ref[...] + ln2b_ref[...]).astype(BF)
        N2[at, :] = n2
        N2T[:, at] = n2.T
        return 0

    lax.fori_loop(0, T // 128, p2b, 0)
    w_1(2, 1)
    w_1(2, 2)
    w_1(2, 3)

    @pl.when(z < NT - 1)
    def _():
        for g in range(NT):
            rcopy(SQ.at[g], SQ.at[g], c_s.at[0, g], c_r.at[0, g], (dp, z)).wait_send()

    UN[...] = jnp.zeros_like(UN)
    GN2[...] = jnp.zeros_like(GN2)
    for copy in local[3:]:
        copy.wait()

    cc = math.sqrt(2.0 / math.pi)

    def p3(j, _):
        g = order(j)

        @pl.when(j == 1)
        def _():
            w_4(1, 1)
            w_2(2, 2)
            w_2(2, 3)
            w_3(2, 1)
            w_3(2, 2)
            w_3(2, 3)
            w_4(2, 1)

        @pl.when(j == 2)
        def _():
            w_4(1, 2)
            w_4(2, 2)

        @pl.when(j == 3)
        def _():
            w_4(1, 3)
            w_4(2, 3)

        def units(u, total):
            pre = dot(N2[...], WB[g, :, col(u)]) + BP[g, pl.ds(1, 1), col(u)]
            sq = pre * pre
            t = jnp.tanh(cc * pre * (1.0 + 0.044715 * sq))
            act = (0.5 * pre * (1.0 + t)).astype(BF)
            slope = 0.5 * (1.0 + t) + (0.5 * cc) * pre * (1.0 - t * t) * (1.0 + (3 * 0.044715) * sq)
            ACT[:, col(u)] = act
            ACTT[col(u), :] = act.T
            gact = dot(cot_ref[...], WC[g, col(u), :], 1, 1)
            gpre = (gact * slope).astype(BF)
            GP[:, col(u)] = gpre
            GBF[g, :, col(u)] = jnp.sum(gpre.astype(F32), axis=0, keepdims=True)
            return total

        lax.fori_loop(0, U // CB, units, 0)

        @pl.when(j == 0)
        def _():
            w_2(2, 1)

        @pl.when(j >= 1)
        def _():
            gp = order(j - 1)
            g_a(1, gp)
            g_a(2, gp)

        def outs(n, _):
            UN[:, col(n)] += dot(ACT[...], WC[g, :, col(n)])
            GN2[:, col(n)] += dot(GP[...], WB[g, col(n), :], 1, 1)
            return 0

        lax.fori_loop(0, D // CB, outs, 0)

        @pl.when(j >= 2)
        def _():
            gp = order(j - 2)
            g_b(1, gp)
            g_b(2, gp)

        def grads(n, _):
            WC[g, col(n), :] = dot(ACTT[col(n), :], cot_ref[...]).astype(BF)
            WB[g, col(n), :] = dot(N2T[col(n), :], GP[...]).astype(BF)
            return 0

        lax.fori_loop(0, D // CB, grads, 0)
        g_core(1, g)
        g_core(2, g)

        @pl.when(j >= 3)
        def _():
            gp = order(j - 3)
            g_z(1, gp)
            g_z(2, gp)

        return 0

    lax.fori_loop(0, NT, p3, 0)

    VS[...] = jnp.zeros_like(VS)

    def p4(i, _):
        at = pl.ds(mo(i * RB_, RB_), RB_)
        mid = MID[at, :]
        res_ref[at, :] = (mid + UN[at, :] + bproj_ref[...]).astype(BF)
        xh, inv = norm_stats(mid)
        gn = GN2[at, :]
        gh = gn * ln2g_ref[...]
        c1 = jnp.mean(gh, axis=-1, keepdims=True)
        c2 = jnp.mean(gh * xh, axis=-1, keepdims=True)
        cot = cot_ref[at, :].astype(F32)
        gm = cot + inv * (gh - c1 - xh * c2)
        GN2[at, :] = gm
        low = gm.astype(BF)
        GML[at, :] = low
        VS[0] += jnp.sum(cot, axis=0, keepdims=True)
        VS[1] += jnp.sum(low.astype(F32), axis=0, keepdims=True)
        VS[2] += jnp.sum(gn * xh, axis=0, keepdims=True)
        VS[3] += jnp.sum(gn, axis=0, keepdims=True)
        return 0

    lax.fori_loop(0, T // RB_, p4, 0)
    g_a(1, order(3))
    g_a(2, order(3))

    tail_row = iota((16, T), 0)

    def p5a(g, _):
        gmix = dot(WA[g, pl.ds(QKV, HC), :], GML[...], 1, 1).astype(BF).astype(F32)
        mix = MX[g]
        WA[g, pl.ds(QKV, HC), :] = dot(mix, GML[...]).astype(BF)
        prod = gmix * mix.astype(F32)
        for h in range(HPG):
            hh = g * HPG + h
            rows = slice(h * HD, (h + 1) * HD)
            inv = DI[hh]
            gden = -jnp.sum(prod[rows], axis=0, keepdims=True) * inv
            hi = gden.astype(BF).astype(F32)
            lo = gden - hi
            tail = jnp.where(tail_row == 0, hi, jnp.where(tail_row == 1, lo, 0.0)).astype(BF)
            ga = jnp.concatenate([(gmix[rows] * inv).astype(BF), tail], axis=0)
            GA[hh] = ga
            gc = dot(ga, QF[hh].T)
            GC[hh] = gc
            SQ[g, h] = gc.astype(BF)

        @pl.when(z == NT - 1)
        def _():
            rcopy(SQ.at[g], GR.at[g], c_s.at[1, g], c_r.at[1, g], (dp, z - 1)).start()

        return 0

    lax.fori_loop(0, NT, p5a, 0)
    g_b(1, order(2))
    g_b(2, order(2))
    g_z(1, order(1))
    g_z(2, order(1))

    def chain_back(g):
        @pl.when(z < NT - 1)
        def _():
            chain_wait(GR, g, 1)
            for h in range(HPG):
                hh = g * HPG + h
                later = jnp.where(from_next, GR[g, h].astype(F32), 0.0)
                SQ[g, h] = (GC[hh] + later).astype(BF)

        @pl.when(jnp.logical_and(z > 0, z < NT - 1))
        def _():
            rcopy(SQ.at[g], GR.at[g], c_s.at[1, g], c_r.at[1, g], (dp, z - 1)).start()

    GN1 = UN
    GN1[...] = jnp.zeros_like(GN1)

    def p5b(g, _):
        chain_back(g)
        gql = []
        gkl = []
        for h in range(HPG):
            hh = g * HPG + h
            qf = QF[hh]
            kf = KF[hh]
            va = VA[hh]
            ga = GA[hh]
            kn = kf.T
            vn = va.T
            ctt = CT[hh].T
            gkc = jnp.where(from_next, GR[g, h], jnp.zeros((AUG, 2 * HD), BF))
            gkt = gkc.T
            gq = [None] * NB
            gk = [None] * NB
            gv = [None] * NB
            for qi in range(NB):
                qs = slice(qi * CB, (qi + 1) * CB)
                gq[qi] = dot(ctt, ga[:, qs])
                for ki in range(qi + 1):
                    ks = slice(ki * CB, (ki + 1) * CB)
                    s = dot(kn[ks], qf[:, qs])
                    gs = dot(vn[ks], ga[:, qs])
                    if ki == qi:
                        s = jnp.where(causal, s, 0.0)
                        gs = jnp.where(causal, gs, 0.0)
                    s = s.astype(BF)
                    gs = gs.astype(BF)
                    gq[qi] = gq[qi] + dot(kf[:, ks], gs)
                    pk = dot(qf[:, qs], gs, 1, 1)
                    pv = dot(ga[:, qs], s, 1, 1)[:HD]
                    gk[ki] = pk if gk[ki] is None else gk[ki] + pk
                    gv[ki] = pv if gv[ki] is None else gv[ki] + pv
            for ki in range(NB):
                ks = slice(ki * CB, (ki + 1) * CB)
                gk[ki] = gk[ki] + dot(gkt, va[:, ks])
                gv[ki] = gv[ki] + dot(gkc[:HD], kf[:, ks])
                GQ[pl.ds(2 * HC + h * HD, HD), ks] = gv[ki].astype(BF)

            def back(feat, grads):
                out = []
                for b in range(NB):
                    bs = slice(b * CB, (b + 1) * CB)
                    p = feat[:HD, bs].astype(F32)
                    m = feat[HD:, bs].astype(F32)
                    g1 = grads[b][:HD]
                    g2 = grads[b][HD:]
                    s1 = jnp.sum(g1 * p, axis=0, keepdims=True)
                    s2 = jnp.sum(g2 * m, axis=0, keepdims=True)
                    out.append((p * (g1 - s1) - m * (g2 - s2)).astype(BF))
                return jnp.concatenate(out, axis=1)

            gql.append(back(qf, gq))
            gkl.append(back(kf, gk))
        comp = None
        for which, parts in ((0, gql), (1, gkl)):
            glog = jnp.concatenate(parts, axis=0)
            own = QK[g, pl.ds(which * HC, HC), :]
            GQ[pl.ds(which * HC, HC), :] = dot(block_diag(g, which), glog, 0, 0).astype(BF)
            gfeat = jnp.where(head_mask, dot(own, glog, 1, 1), 0.0).astype(BF)
            part = dot(gfeat, pick_back(which))
            comp = part if comp is None else comp + part
        comp = comp.astype(BF)
        gq_all = GQ[...]
        gqn = gq_all[:QKV].T
        for n in range(D // CB):
            GN1[:, n * CB : (n + 1) * CB] += dot(gqn, WA[g, pl.ds(0, QKV), n * CB : (n + 1) * CB])
        WA[g, pl.ds(0, QKV), :] = dot(gq_all[:QKV], N1[...]).astype(BF)
        for b in range(HC // 32):
            WA[g, pl.ds(D, 32), b * 128 : (b + 1) * 128] = comp[b * 32 : (b + 1) * 32]
        vec = dot(ones_rows, gq_all, 1, 1)
        row = iota((16, D), 0)
        vec = jnp.where(row == 1, GBF[g], vec)
        for i in range(4):
            vec = jnp.where(row == 2 + i, VS[i], vec)
        WA[g, pl.ds(D + 32, 16), :] = vec.astype(BF)
        g_core(0, g)

        @pl.when(g == 0)
        def _():
            g_b(1, order(3))
            g_b(2, order(3))
            g_z(1, order(2))
            g_z(2, order(2))

        @pl.when(g == 1)
        def _():
            g_z(1, order(3))
            g_z(2, order(3))

        @pl.when(g >= 1)
        def _():
            g_a(0, g - 1)

        @pl.when(g >= 2)
        def _():
            g_b(0, g - 2)

        @pl.when(g >= 3)
        def _():
            g_z(0, g - 3)
            g_sum(1)
            g_sum(2)

        return 0

    lax.fori_loop(0, NT, p5b, 0)
    g_a(0, NT - 1)

    LS[...] = jnp.zeros_like(LS)

    def p6(i, _):
        at = pl.ds(mo(i * RB_, RB_), RB_)
        xh, inv = norm_stats(x_ref[at, :].astype(F32))
        gn = GN1[at, :]
        gh = gn * ln1g_ref[...]
        c1 = jnp.mean(gh, axis=-1, keepdims=True)
        c2 = jnp.mean(gh * xh, axis=-1, keepdims=True)
        gin_ref[at, :] = (GN2[at, :] + inv * (gh - c1 - xh * c2)).astype(BF)
        LS[0, 0:1, :] += jnp.sum(gn * xh, axis=0, keepdims=True)
        LS[0, 1:2, :] += jnp.sum(gn, axis=0, keepdims=True)
        return 0

    lax.fori_loop(0, T // RB_, p6, 0)

    partners = [dp + d_core, dp + d_x, dp + d_y] + [high(i) for i in range(nh)]

    def small_sum(i):
        copy = rcopy(LS.at[i], LR.at[i], l_s.at[i], l_r.at[i], (partners[i], z))
        copy.start()
        copy.wait()
        LS[i + 1] = LS[i] + LR[i]

    g_b(0, NT - 2)
    g_z(0, NT - 3)
    o_2(1)
    o_2(2)
    for i in range(len(partners)):
        small_sum(i)
    last = len(partners)
    g_b(0, NT - 1)
    g_z(0, NT - 2)
    o_3(1)
    o_3(2)
    LZ[z] = LS[last]
    for o in range(1, NT):
        rcopy(LS.at[last], LZ.at[z], lz_s.at[o - 1], lz_r.at[z], (dp, lax.rem(z + o, NT))).start()
    g_z(0, NT - 1)
    outs = [o_4(1, ob_ref, own_s.at[0]), o_4(2, oc_ref, own_s.at[1])]
    g_sum(0)
    for o in range(1, NT):
        zz = lax.rem(z + o, NT)
        rcopy(LZ.at[zz], LZ.at[zz], lz_s.at[o - 1], lz_r.at[zz], (dp, z)).wait_recv()
    total = LZ[0]
    for zz in range(1, NT):
        total = total + LZ[zz]
    ov_ref[...] = total
    o_2(0)
    o_3(0)
    outs.append(o_4(0, oa_ref, own_s.at[2]))
    for copy in outs:
        copy.wait()

    for o in range(1, NT):
        rcopy(LS.at[last], LZ.at[z], lz_s.at[o - 1], lz_r.at[z], (dp, lax.rem(z + o, NT))).wait_send()
    small_done()
    for k in range(KINDS):
        w_z_done(k)
        for g in range(NT):
            g_done(k, g)

    @pl.when(z > 0)
    def _():
        for g in range(NT):
            rcopy(SQ.at[g], SQ.at[g], c_s.at[1, g], c_r.at[1, g], (dp, z)).wait_send()


def layer_call(nh, T, *args):
    def vm(shape, dtype=BF):
        return pltpu.VMEM(shape, dtype)

    dma = pltpu.SemaphoreType.DMA
    nhb = max(nh, 1)
    nst = 3 + nh
    scratch = [
        vm((NT, ROWS_G[0], D)),
        vm((NT, D, U)),
        vm((NT, U, D)),
        vm((NT, HC, 2 * HD)),
        vm((NT, 8, D), F32),
    ]
    scratch += [vm((NT, 4 * r, D)) for r in R_G]
    scratch += [vm((NT, 2, r, D)) for r in R_G]
    scratch += [vm((NT, r, D)) for r in R_G]
    scratch += [vm((NT, r, D)) for r in R_G]
    scratch += [vm((rows, D)) for rows in ROWS_G]
    scratch += [vm((nhb, r if nh else 16, D)) for r in R_G]
    scratch += [vm((nst + 1, 8, D), F32), vm((nst, 8, D), F32), vm((NT, 8, D), F32)]
    scratch += [
        vm((T, D)),
        vm((NT, 2 * HC, T)),
        vm((NH, AUG, T)),
        vm((NH, 2 * HD, T)),
        vm((NH, 2 * HD, T)),
        vm((NH, HD + 8, T), F32),
        vm((NH, AUG, 2 * HD), F32),
        vm((NH, AUG, 2 * HD)),
        vm((NT, HPG, AUG, 2 * HD)),
        vm((NT, HPG, AUG, 2 * HD)),
        vm((NT, HPG, AUG, 2 * HD)),
        vm((NT, HC, T)),
        vm((NH, 1, T), F32),
        vm((T, D), F32),
        vm((T, D)),
        vm((D, T)),
        vm((T, D), F32),
        vm((T, D), F32),
        vm((T, D)),
        vm((T, U)),
        vm((U, T)),
        vm((T, U)),
        vm((NT, 1, U), F32),
        vm((NH, AUG, T)),
        vm((NH, AUG, 2 * HD), F32),
        vm((D, T)),
        vm((4, 1, D), F32),
    ]
    scratch += [
        dma((5,)),
        dma((2, NT - 1)),
        dma((2, NT)),
        dma((KINDS, NT - 1)),
        dma((4, KINDS, NT)),
        dma((5, KINDS, NT)),
        dma((5, KINDS, NT)),
        dma((4, KINDS, NT)),
        dma((KINDS, NT)),
        dma((4, KINDS)),
        dma((4, KINDS)),
        dma((nhb, KINDS)),
        dma((nhb, KINDS)),
        dma((nst,)),
        dma((nst,)),
        dma((NT - 1,)),
        dma((NT,)),
        dma((2, NT)),
        dma((2, NT)),
    ]
    vmem = pl.BlockSpec(memory_space=pltpu.VMEM)
    hbm = pl.BlockSpec(memory_space=pl.ANY)
    return pl.pallas_call(
        functools.partial(layer_kernel, nh),
        out_shape=(
            jax.ShapeDtypeStruct((T, D), BF),
            jax.ShapeDtypeStruct((T, D), BF),
            jax.ShapeDtypeStruct((ROWS_G[0], D), BF),
            jax.ShapeDtypeStruct((D, U), BF),
            jax.ShapeDtypeStruct((U, D), BF),
            jax.ShapeDtypeStruct((8, D), F32),
        ),
        in_specs=[pl.BlockSpec(memory_space=pltpu.SMEM)] + [vmem] * 8 + [hbm] * 5,
        out_specs=(vmem, vmem, hbm, hbm, hbm, vmem),
        scratch_shapes=scratch,
        compiler_params=pltpu.CompilerParams(
            collective_id=0, has_side_effects=True, vmem_limit_bytes=67043328
        ),
    )(*args)


def local(
    nh,
    tokens_in,
    ln1_gain,
    ln1_bias,
    w_qkv,
    b_qkv,
    feat_q,
    feat_k,
    w_out,
    b_out,
    ln2_gain,
    ln2_bias,
    w_fc,
    b_fc,
    w_proj,
    b_proj,
    seq_lengths,
    cotangent,
):
    T = tokens_in.shape[0]
    a_own = jnp.concatenate([jnp.transpose(w_qkv, (1, 2, 0)).reshape(QKV, D), w_out], axis=0)
    ft_own = jnp.concatenate(
        [jnp.transpose(feat_q, (0, 2, 1)).reshape(HC, HD), jnp.transpose(feat_k, (0, 2, 1)).reshape(HC, HD)],
        axis=1,
    )
    bq = jnp.pad(b_qkv.reshape(1, QKV), ((0, 0), (0, D - QKV)))
    bp_own = jnp.concatenate([bq, b_fc.reshape(1, U), jnp.zeros((6, D), F32)], axis=0)

    def row(v):
        return v.reshape(1, D)

    res, gin, oa, ob, oc, ov = layer_call(
        nh,
        T,
        seq_lengths,
        tokens_in,
        cotangent,
        row(ln1_gain),
        row(ln1_bias),
        row(b_out),
        row(ln2_gain),
        row(ln2_bias),
        row(b_proj),
        a_own,
        w_fc,
        w_proj,
        ft_own,
        bp_own,
    )
    g_w_qkv = jnp.transpose(oa[:QKV].reshape(3, HC, D), (2, 0, 1)).astype(F32)
    g_w_out = oa[QKV:D].astype(F32)
    feats = jnp.transpose(oa[D : D + 32].reshape(32, HC // 32, 2 * HD), (1, 0, 2)).reshape(HC, 2 * HD)
    feats = feats.astype(F32).reshape(HPG, HD, 2 * HD)
    vec = oa[D + 32 : D + 48].astype(F32)
    return (
        res,
        gin,
        ov[0],
        ov[1],
        g_w_qkv,
        vec[0, :QKV].reshape(3, HC),
        feats[:, :, :HD],
        feats[:, :, HD:],
        g_w_out,
        vec[3],
        vec[4],
        vec[5],
        ob.astype(F32),
        vec[1],
        oc.astype(F32),
        vec[2],
    )


def solution(mesh):
    n_dp = mesh.shape["dp"]
    nh = max(0, (n_dp // 8).bit_length() - 1)
    return jax.shard_map(
        functools.partial(local, nh),
        mesh=mesh,
        in_specs=(
            P(("dp", "tensor"), None),
            P(),
            P(),
            P(None, None, "tensor"),
            P(None, "tensor"),
            P("tensor", None, None),
            P("tensor", None, None),
            P("tensor", None),
            P(),
            P(),
            P(),
            P(None, "tensor"),
            P("tensor"),
            P("tensor", None),
            P(),
            P("dp", None),
            P(("dp", "tensor"), None),
        ),
        out_specs=(
            P(("dp", "tensor"), None),
            P(("dp", "tensor"), None),
            P(),
            P(),
            P(None, None, "tensor"),
            P(None, "tensor"),
            P("tensor", None, None),
            P("tensor", None, None),
            P("tensor", None),
            P(),
            P(),
            P(),
            P(None, "tensor"),
            P("tensor"),
            P("tensor", None),
            P(),
        ),
        check_vma=False,
    )
```

time: 924 us -> 262 us (0.28)
  waiting for transfers between devices: 580 us -> 0 us
  Pallas kernels: 0 us -> 228 us
  matrix products: 103 us -> 0 us
  other arithmetic: 101 us -> 11.7 us
  local copies, waits for them, and re-layouts: 71.2 us -> 16.7 us
  blocking collectives: 40.8 us -> 0 us
  between operations: 16.9 us -> 0.72 us
    all_gather x4 -> x0, waiting for transfers between devices: 243 us -> none  [the longest x1 62.9 us: local(): gathered_two = lax.all_gather(normed_two, 'tensor', axis=0, tiled=True)]
    pallas_call x0 -> x1, Pallas kernels: none -> 228 us  [layer_call(): pl.pallas_call(functools.partial(layer_kernel, nh), out_shape=(jax.ShapeD...]
    reduce_scatter x4 -> x0, waiting for transfers between devices: 207 us -> none  [the longest x1 59.9 us: local(): lax.psum_scatter(jnp.dot(act_low, w_proj, preferred_element_type=jnp.floa...]
    psum x2 -> x0, waiting for transfers between devices: 129 us -> none  [local(): lax.psum((grad_w_qkv, grad_b_qkv, grad_feat_q, grad_feat_k, grad_w_out, g...]
    dot_general x34 -> x0, matrix products: 93.3 us -> none  [the longest x1 12.6 us: local(): jnp.einsum('rd,fd->rf', grad_out_all, w_proj, preferred_element_type=jnp....]
    psum x1 -> x0, blocking collectives: 40.8 us -> none  [local(): lax.psum((grad_ln1_gain, grad_ln1_bias, grad_b_out, grad_ln2_gain, grad_l...]
    sub x4 -> x0, other arithmetic: 39.9 us -> none  [the longest x2 20.1 us: feature(): jax.nn.softmax(-logits, axis=-1)]
    reduce_sum x15 -> x0, other arithmetic: 34.2 us -> none  [the longest x2 9.16 us: feature(): jax.nn.softmax(-logits, axis=-1)]
  transfers between devices with their start and end apart: 10 -> 0, of which waited for: 10 -> 0; matrix products, arithmetic and copies ran while one was open for 5% -> 0% of each run, Pallas kernels for 0% -> 0%
where the time goes in v1:
time: 262 us; the launch traced here: 257 us
  Pallas kernels  228 us (87%)
  local copies, waits for them, and re-layouts  16.7 us (6%)
  other arithmetic  11.7 us (4%)
    pallas_call x1, Pallas kernels, layer_call(): pl.pallas_call(functools.partial(layer_kernel, nh), out_shape=(jax.ShapeD...  228 us
    reshape x6, local copies, waits for them, and re-layouts, row(): return v.reshape(1, D)  7.6 us

profile of v1, /device:TPU:1, one launch (start us, length us, event | category | flops | bytes accessed | tf_op | source)
XLA Modules:
  0.0 257.3 jit_solution(15390562004545936759)
XLA Ops:
  0.7 0.1 pad.7.clone
  0.7 0.8 reshape.85
  1.5 1.3 reshape.76.ln1g_ref
  2.8 1.3 reshape.77.ln1b_ref
  4.0 1.3 reshape.78.bout_ref
  5.3 1.3 reshape.79.ln2g_ref
  6.6 1.3 reshape.80.ln2b_ref
  7.8 0.7 reshape.86
  8.5 1.3 reshape.81.bproj_ref
  9.8 0.7 fusion.bp_own
  10.5 0.9 copy.38
  11.4 0.9 copy.39
  12.3 0.7 pad_maximum_fusion.1.ft_own
  13.0 2.4 pad_maximum_fusion.a_own
  15.3 228.2 %shard_map.288 = (bf16[512,768]{1,0:T(8,128)(2,1)}, bf16[512,768]{1,0:T(8,128)(2,1)}, bf16[896,768]{1,0:T(8,128)(2,1)}, bf16[768,768]{1,0:T(8,128)(2,1)}, bf16[768,768]{1,0:T(8,128)(2,1)}, /*index=5*/f32[8,768]{1,0:T(8,128)}) custom-call(s32[1,2]{1,0:T(1,128)} %seq_ref.1, bf16[512,768]{1,0:T(8,128)(2,1)} %x_ref.1, bf16[512,768]{1,0:T(8,128)(2,1)} %cot_ref.1, ...), custom_call_target="tpu_custom_call" | custom-call | tf_op jit(solution)/shard_map/pallas_call | solution.py:1017
  243.5 0.0 copy-start.2
  243.5 0.8 slice_convert_fusion.2
  244.4 1.5 slice_reduce_fusion
  245.9 0.7 reshape_squeeze.3
  246.5 0.8 slice_convert_fusion.1
  247.4 0.7 fusion.1
  248.1 1.8 slice_convert_fusion
  250.0 0.1 slice.44
  250.0 0.0 copy-start.1
  250.0 1.4 convert_bitcast_fusion
  251.4 0.4 copy-done.1
  251.7 1.6 convert_element_type.45
  253.3 0.1 copy-done
  253.4 1.6 convert_element_type.46
  255.0 0.9 copy.43
  255.9 0.5 copy-done.3
  256.4 0.9 copy.44
  (9 shorter events, 0.1 us)
Async XLA Ops:
  243.5 6.5 %copy-start.2 = (bf16[896,768]{1,0:T(8,128)(2,1)S(1)}, bf16[896,768]{1,0:T(8,128)(2,1)}, u32[]{:S(2)}) copy-start(bf16[896,768]{1,0:T(8,128)(2,1)} %get-tuple-element.25) | copy-start | bytes 4128772
  250.0 1.7 copy-start.1
  251.7 1.7 copy-start
  253.4 1.6 copy-start.4
  255.0 1.4 copy-start.3

commit v2 on v1

--- a/solution.py
+++ b/solution.py
@@ -26,6 +26,8 @@
 R_G = (112, 96, 96)
 ROWS_G = (896, 768, 768)
 CB = 256
+HALF_W = (48, 48)
+HALF_G = ((64, 48), (48, 48), (48, 48))
 
 
 def dot(a, b, ca=1, cb=0):
@@ -174,8 +176,14 @@
     O = (OA, OB, OC)
     RH = (RHA, RHB, RHC)
 
-    def order(j):
-        return jnp.where(j == 0, z, j - 1 + (j - 1 >= z).astype(jnp.int32))
+    def flip(j):
+        return lax.rem(z // 2 + j // 2, 2) * 2 + lax.rem(z + j, 2)
+
+    def ff(j):
+        return flip(lax.rem(NT - j, NT))
+
+    def last(t):
+        return flip(NT - 1 - t)
 
     def high(i):
         step = 8 * 2**i
@@ -186,34 +194,12 @@
             src_ref=src, dst_ref=dst, send_sem=ssem, recv_sem=rsem, device_id=dev, device_id_type=MESH
         )
 
-    def first_is_y(k, g):
-        return lax.rem(k + g, 2)
-
-    def step_a(k, g):
-        q = first_is_y(k, g)
-        return dp + q * d_y + (1 - q) * d_x
-
-    def step_b(k, g):
-        q = first_is_y(k, g)
-        return dp + q * d_x + (1 - q) * d_y
-
-    def slot_of(k, g, flip_a, flip_b):
-        q = first_is_y(k, g)
-        sx = bx + (1 - 2 * bx) * (q * flip_b + (1 - q) * flip_a)
-        sy = by + (1 - 2 * by) * (q * flip_a + (1 - q) * flip_b)
-        return core * 4 + sy * 2 + sx
-
-    def abs_slot(k, g, flip_a, bit_b):
-        q = first_is_y(k, g)
-        ax = bx + (1 - 2 * bx) * flip_a
-        ay = by + (1 - 2 * by) * flip_a
-        sx = q * bit_b + (1 - q) * ax
-        sy = q * ay + (1 - q) * bit_b
-        return core * 4 + sy * 2 + sx
-
-    def my_b_bit(k, g):
-        q = first_is_y(k, g)
-        return q * bx + (1 - q) * by
+    dev_x = (dp + d_x, z)
+    dev_y = (dp + d_y, z)
+    dev_c = (dp + d_core, z)
+    slot_x = core * 4 + by * 2 + (1 - bx)
+    slot_y = core * 4 + (1 - by) * 2 + bx
+    slot_d = core * 4 + (1 - by) * 2 + (1 - bx)
 
     peers = [(dp + d_core, z), (dp + d_x, z), (dp + d_y, z)]
     peers += [(high(i), z) for i in range(nh)]
@@ -229,52 +215,48 @@
     def wrows4(k, g, c):
         return W[k].at[g, pl.ds(mo(c * 4 * R_W, R_W), 4 * R_W), :]
 
-    def w_z(k):
-        for o in range(1, NT):
-            rcopy(
-                OWN[k].at[pl.ds(mo(slot * R_W, R_W), R_W), :],
-                wrows(k, z, slot),
-                wz_s.at[k, o - 1],
-                w_r.at[0, k, z],
-                (dp, lax.rem(z + o, NT)),
-            ).start()
+    def whalf(k, g, s, h):
+        return W[k].at[g, pl.ds(mo(s * R_W + h * HALF_W[0], 16), HALF_W[h]), :]
+
+    def w_z(k, g):
+        rcopy(
+            OWN[k].at[pl.ds(mo(slot * R_W, R_W), R_W), :], wrows(k, z, slot), wz_s.at[k, g], w_r.at[0, k, z], (dp, g)
+        ).start()
 
     def w_wait(k, g, stage, ref):
-        rcopy(ref, ref, w_s.at[0, k, g], w_r.at[stage, k, g], (dp + d_core, z)).wait_recv()
-
-    def w_1(k, i):
-        g = order(i)
-        w_wait(k, g, 0, wrows(k, g, slot))
-        src = wrows(k, g, slot)
-        rcopy(src, src, w_s.at[0, k, g], w_r.at[1, k, g], (step_a(k, g), z)).start()
-
-    def w_2(k, i):
-        g = order(i)
-        w_wait(k, g, 1, wrows(k, g, slot_of(k, g, 1, 0)))
-        for f in range(2):
-            src = wrows(k, g, slot_of(k, g, f, 0))
-            rcopy(src, src, w_s.at[1 + f, k, g], w_r.at[2 + f, k, g], (step_b(k, g), z)).start()
-
-    def w_3(k, i):
-        g = order(i)
-        for f in range(2):
-            w_wait(k, g, 2 + f, wrows(k, g, slot_of(k, g, f, 1)))
-        src = wrows4(k, g, core)
-        rcopy(src, src, w_s.at[3, k, g], w_r.at[4, k, g], (dp + d_core, z)).start()
-
-    def w_4(k, i):
-        g = order(i)
-        w_wait(k, g, 4, wrows4(k, g, 1 - core))
-        one = wrows(k, g, slot)
-        for st in range(3):
-            rcopy(one, one, w_s.at[st, k, g], w_r.at[0, k, g], (dp + d_core, z)).wait_send()
-        four = wrows4(k, g, core)
-        rcopy(four, four, w_s.at[3, k, g], w_r.at[0, k, g], (dp + d_core, z)).wait_send()
+        rcopy(ref, ref, w_s.at[0, k, g], w_r.at[stage, k, g], dev_c).wait_recv()
+
+    def w_send(k, g, s_stage, r_stage, ref, dev):
+        rcopy(ref, ref, w_s.at[s_stage, k, g], w_r.at[r_stage, k, g], dev).start()
+
+    def w_1(k, g):
+        mine = wrows(k, g, slot)
+        w_wait(k, g, 0, mine)
+        w_send(k, g, 0, 1, mine, dev_x)
+        w_send(k, g, 1, 2, mine, dev_y)
+
+    def w_2(k, g):
+        w_wait(k, g, 1, wrows(k, g, slot_x))
+        w_send(k, g, 2, 3, whalf(k, g, slot_x, 0), dev_y)
+        w_wait(k, g, 2, wrows(k, g, slot_y))
+        w_send(k, g, 3, 4, whalf(k, g, slot_y, 1), dev_x)
+
+    def w_3(k, g):
+        w_wait(k, g, 3, whalf(k, g, slot_d, 0))
+        w_wait(k, g, 4, whalf(k, g, slot_d, 1))
+        w_send(k, g, 4, 5, wrows4(k, g, core), dev_c)
+
+    def w_4(k, g):
+        w_wait(k, g, 5, wrows4(k, g, 1 - core))
+        sent = [wrows(k, g, slot)] * 2 + [whalf(k, g, slot_x, 0), whalf(k, g, slot_y, 1), wrows4(k, g, core)]
+        for st, ref in enumerate(sent):
+            rcopy(ref, ref, w_s.at[st, k, g], w_r.at[0, k, g], dev_c).wait_send()
 
     def w_z_done(k):
         one = OWN[k].at[pl.ds(mo(slot * R_W, R_W), R_W), :]
-        for o in range(1, NT):
-            rcopy(one, one, wz_s.at[k, o - 1], w_r.at[0, k, z], (dp, lax.rem(z + o, NT))).wait_send()
+        for i in range(1, NT):
+            g = flip(i)
+            rcopy(one, wrows(k, z, slot), wz_s.at[k, g], w_r.at[0, k, z], (dp, g)).wait_send()
 
     small = ((ft_own, FT), (bp_own, BP))
 
@@ -300,9 +282,13 @@
         pltpu.make_async_copy(c_own, WC.at[z], own_s.at[4]),
     ]
     small_send()
-    w_z(0)
+    for i in range(1, NT):
+        w_z(0, flip(i))
     for copy in local:
         copy.start()
+    for j in range(1, NT):
+        w_z(1, ff(j))
+        w_z(2, ff(j))
 
     def grows(k, g, s, n=1):
         return W[k].at[g, pl.ds(mo(s * R_G[k], 16), n * R_G[k]), :]
@@ -317,62 +303,65 @@
 
         lax.fori_loop(0, n // blk, body, 0)
 
+    def ghalf(k, g, s, h):
+        return W[k].at[g, pl.ds(mo(s * R_G[k] + h * HALF_G[k][0], 16), HALF_G[k][h]), :]
+
+    def ra(k, g, h):
+        return RA[k].at[g, pl.ds(h * HALF_G[k][0], HALF_G[k][h]), :]
+
     def g_wait(k, g, stage, ref):
-        rcopy(ref, ref, g_s.at[0, k, g], g_r.at[stage, k, g], (dp + d_core, z)).wait_recv()
+        rcopy(ref, ref, g_s.at[0, k, g], g_r.at[stage, k, g], dev_c).wait_recv()
+
+    def g_send(k, g, stage, src, dst, dev):
+        rcopy(src, dst, g_s.at[stage, k, g], g_r.at[stage, k, g], dev).start()
 
     def g_core(k, g):
-        rcopy(
-            grows(k, g, (1 - core) * 4, 4), R0[k].at[g], g_s.at[0, k, g], g_r.at[0, k, g], (dp + d_core, z)
-        ).start()
+        g_send(k, g, 0, grows(k, g, (1 - core) * 4, 4), R0[k].at[g], dev_c)
 
     def g_a(k, g):
         g_wait(k, g, 0, R0[k].at[g])
         add_rows(W[k].at[g], core * 4 * R_G[k], R0[k].at[g], 4 * R_G[k])
-        for b in range(2):
-            rcopy(
-                grows(k, g, abs_slot(k, g, 1, b)),
-                RA[k].at[g, b],
-                g_s.at[1 + b, k, g],
-                g_r.at[1 + b, k, g],
-                (step_a(k, g), z),
-            ).start()
+        g_send(k, g, 1, ghalf(k, g, slot_d, 0), ra(k, g, 0), dev_x)
+        g_send(k, g, 2, ghalf(k, g, slot_d, 1), ra(k, g, 1), dev_y)
 
     def g_b(k, g):
-        for b in range(2):
-            g_wait(k, g, 1 + b, RA[k].at[g, b])
-            add_rows(W[k].at[g], abs_slot(k, g, 0, b) * R_G[k], RA[k].at[g, b], R_G[k])
-        rcopy(
-            grows(k, g, slot_of(k, g, 0, 1)),
-            RB[k].at[g],
-            g_s.at[3, k, g],
-            g_r.at[3, k, g],
-            (step_b(k, g), z),
-        ).start()
+        g_wait(k, g, 1, ra(k, g, 0))
+        add_rows(W[k].at[g], slot_y * R_G[k], ra(k, g, 0), HALF_G[k][0])
+        g_send(k, g, 4, grows(k, g, slot_y), RB[k].at[g, 1], dev_y)
+        g_wait(k, g, 2, ra(k, g, 1))
+        add_rows(W[k].at[g], slot_x * R_G[k] + HALF_G[k][0], ra(k, g, 1), HALF_G[k][1])
+        g_send(k, g, 3, grows(k, g, slot_x), RB[k].at[g, 0], dev_x)
 
     def g_z(k, g):
-        g_wait(k, g, 3, RB[k].at[g])
-        add_rows(W[k].at[g], slot * R_G[k], RB[k].at[g], R_G[k])
+        for i in range(2):
+            g_wait(k, g, 3 + i, RB[k].at[g, i])
+            add_rows(W[k].at[g], slot * R_G[k], RB[k].at[g, i], R_G[k])
 
         @pl.when(g != z)
         def _():
-            rcopy(grows(k, g, slot), ZR[k].at[z], g_s.at[4, k, g], z_r.at[k, z], (dp, g)).start()
+            rcopy(grows(k, g, slot), ZR[k].at[z], g_s.at[5, k, g], z_r.at[k, z], (dp, g)).start()
 
     def g_done(k, g):
-        four = grows(k, g, 0, 4)
         one = grows(k, g, 0)
-        rcopy(four, four, g_s.at[0, k, g], g_r.at[0, k, g], (dp + d_core, z)).wait_send()
-        for st in range(1, 4):
-            rcopy(one, one, g_s.at[st, k, g], g_r.at[0, k, g], (dp + d_core, z)).wait_send()
+        sent = [grows(k, g, 0, 4), ghalf(k, g, 0, 0), ghalf(k, g, 0, 1), one, one]
+        for st, ref in enumerate(sent):
+            rcopy(ref, ref, g_s.at[st, k, g], g_r.at[0, k, g], dev_c).wait_send()
 
         @pl.when(g != z)
         def _():
-            rcopy(one, one, g_s.at[4, k, g], g_r.at[0, k, g], (dp + d_core, z)).wait_send()
+            rcopy(one, one, g_s.at[5, k, g], g_r.at[0, k, g], dev_c).wait_send()
 
     def orows(k, s, n=1):
         return O[k].at[pl.ds(mo(s * R_G[k], 16), n * R_G[k]), :]
 
+    def ohalf(k, s, h):
+        return O[k].at[pl.ds(mo(s * R_G[k] + h * HALF_G[k][0], 16), HALF_G[k][h]), :]
+
     def o_wait(k, stage, ref):
-        rcopy(ref, ref, o_s.at[stage, k], o_r.at[stage, k], (dp + d_core, z)).wait_recv()
+        rcopy(ref, ref, o_s.at[stage, k], o_r.at[stage, k], dev_c).wait_recv()
+
+    def o_send(k, stage, ref, dev):
+        rcopy(ref, ref, o_s.at[stage, k], o_r.at[stage, k], dev).start()
 
     def g_sum(k):
         for o in range(1, NT):
@@ -395,30 +384,27 @@
             rcopy(orows(k, slot), RH[k].at[i], h_s.at[i, k], h_r.at[i, k], (high(i), z)).start()
             rcopy(orows(k, slot), RH[k].at[i], h_s.at[i, k], h_r.at[i, k], (high(i), z)).wait()
             add_rows(O[k], slot * R_G[k], RH[k].at[i], R_G[k])
-        src = orows(k, slot)
-        rcopy(src, src, o_s.at[0, k], o_r.at[0, k], (step_b(k, z), z)).start()
+        o_send(k, 0, orows(k, slot), dev_x)
+        o_send(k, 1, orows(k, slot), dev_y)
 
     def o_2(k):
-        o_wait(k, 0, orows(k, slot_of(k, z, 0, 1)))
-        for f in range(2):
-            src = orows(k, slot_of(k, z, 0, f))
-            rcopy(src, src, o_s.at[1 + f, k], o_r.at[1 + f, k], (step_a(k, z), z)).start()
+        o_wait(k, 0, orows(k, slot_x))
+        o_send(k, 2, ohalf(k, slot_x, 0), dev_y)
+        o_wait(k, 1, orows(k, slot_y))
+        o_send(k, 3, ohalf(k, slot_y, 1), dev_x)
 
     def o_3(k):
-        for f in range(2):
-            o_wait(k, 1 + f, orows(k, slot_of(k, z, 1, f)))
-        src = orows(k, core * 4, 4)
-        rcopy(src, src, o_s.at[3, k], o_r.at[3, k], (dp + d_core, z)).start()
+        o_wait(k, 2, ohalf(k, slot_d, 0))
+        o_wait(k, 3, ohalf(k, slot_d, 1))
+        o_send(k, 4, orows(k, core * 4, 4), dev_c)
 
     def o_4(k, out, sem):
-        o_wait(k, 3, orows(k, (1 - core) * 4, 4))
+        o_wait(k, 4, orows(k, (1 - core) * 4, 4))
         copy = pltpu.make_async_copy(O[k], out, sem)
         copy.start()
-        one = orows(k, slot)
-        for st in range(3):
-            rcopy(one, one, o_s.at[st, k], o_r.at[0, k], (dp + d_core, z)).wait_send()
-        four = orows(k, core * 4, 4)
-        rcopy(four, four, o_s.at[3, k], o_r.at[0, k], (dp + d_core, z)).wait_send()
+        sent = [orows(k, slot)] * 2 + [ohalf(k, slot_x, 0), ohalf(k, slot_y, 1), orows(k, core * 4, 4)]
+        for st, ref in enumerate(sent):
+            rcopy(ref, ref, o_s.at[st, k], o_r.at[0, k], dev_c).wait_send()
         return copy
 
     def iota(shape, axis):
@@ -475,36 +461,31 @@
         copy.wait()
 
     def p1(j, _):
-        g = order(j)
+        g = flip(j)
 
         @pl.when(j == 1)
         def _():
-            small_wait(order(1))
-            w_1(0, 1)
-            w_1(0, 2)
-            w_2(0, 1)
-            w_1(0, 3)
-            w_z(1)
-            w_2(0, 2)
-            w_3(0, 1)
-            w_2(0, 3)
-            w_3(0, 2)
-            w_4(0, 1)
+            small_wait(flip(1))
+            w_1(0, flip(1))
+            w_2(0, flip(1))
+            w_1(0, flip(2))
+            w_1(0, flip(3))
+            w_3(0, flip(1))
+            w_2(0, flip(2))
+            w_4(0, flip(1))
 
         @pl.when(j == 2)
         def _():
-            small_wait(order(2))
-            w_3(0, 3)
-            w_4(0, 2)
+            small_wait(flip(2))
+            w_2(0, flip(3))
+            w_3(0, flip(2))
+            w_4(0, flip(2))
 
         @pl.when(j == 3)
         def _():
-            small_wait(order(3))
-            w_4(0, 3)
-            w_1(1, 1)
-            w_1(1, 2)
-            w_1(1, 3)
-            w_z(2)
+            small_wait(flip(3))
+            w_3(0, flip(3))
+            w_4(0, flip(3))
 
         bias = jnp.transpose(BP[g])[:QKV, 0:1]
         qkv = (dot(WA[g, pl.ds(0, QKV), :], N1[...], 1, 1) + bias).astype(BF)
@@ -533,12 +514,18 @@
                     part = dot(va[:, ks], s.astype(BF))
                     acc = part if acc is None else acc + part
                 NM[hh, :, qs] = acc[: HD + 8]
+
+        @pl.when(z == 0)
+        def _():
+            for h in range(HPG):
+                SQ[g, h] = ST[g * HPG + h].astype(BF)
+            rcopy(SQ.at[g], CR.at[g], c_s.at[0, g], c_r.at[0, g], (dp, z + 1)).start()
+
         return 0
 
     lax.fori_loop(0, NT, p1, 0)
-    w_2(1, 1)
-    w_2(1, 2)
-    w_2(1, 3)
+    w_1(1, ff(1))
+    w_1(2, ff(1))
 
     def chain_wait(buf, g, stage):
         rcopy(buf.at[g], buf.at[g], c_s.at[stage, g], c_r.at[stage, g], (dp, z)).wait_recv()
@@ -549,15 +536,22 @@
             chain_wait(CR, g, 0)
 
         for h in range(HPG):
-            hh = g * HPG + h
-            carried = jnp.where(from_prev, CR[g, h].astype(F32), 0.0)
-            SQ[g, h] = (ST[hh] + carried).astype(BF)
-            CT[hh] = carried.astype(BF)
-
-        @pl.when(z < NT - 1)
-        def _():
+            CT[g * HPG + h] = jnp.where(from_prev, CR[g, h], jnp.zeros((AUG, 2 * HD), BF))
+
+        @pl.when(jnp.logical_and(z > 0, z < NT - 1))
+        def _():
+            for h in range(HPG):
+                hh = g * HPG + h
+                SQ[g, h] = (ST[hh] + CT[hh].astype(F32)).astype(BF)
             rcopy(SQ.at[g], CR.at[g], c_s.at[0, g], c_r.at[0, g], (dp, z + 1)).start()
 
+        return 0
+
+    lax.fori_loop(0, NT, p1b, 0)
+    w_2(1, ff(1))
+    w_2(2, ff(1))
+
+    def p1c(g, _):
         for h in range(HPG):
             hh = g * HPG + h
             num = NM[hh] + dot(CT[hh], QF[hh])[: HD + 8]
@@ -566,10 +560,7 @@
             MX[g, pl.ds(h * HD, HD), :] = (num[:HD] * inv).astype(BF)
         return 0
 
-    lax.fori_loop(0, NT, p1b, 0)
-    w_3(1, 1)
-    w_3(1, 2)
-    w_3(1, 3)
+    lax.fori_loop(0, NT, p1c, 0)
 
     def p2(n, _):
         acc = None
@@ -590,9 +581,10 @@
         return 0
 
     lax.fori_loop(0, T // 128, p2b, 0)
-    w_1(2, 1)
-    w_1(2, 2)
-    w_1(2, 3)
+    w_3(1, ff(1))
+    w_3(2, ff(1))
+    w_1(1, ff(2))
+    w_1(2, ff(2))
 
     @pl.when(z < NT - 1)
     def _():
@@ -607,27 +599,24 @@
     cc = math.sqrt(2.0 / math.pi)
 
     def p3(j, _):
-        g = order(j)
+        g = ff(j)
 
         @pl.when(j == 1)
         def _():
-            w_4(1, 1)
-            w_2(2, 2)
-            w_2(2, 3)
-            w_3(2, 1)
-            w_3(2, 2)
-            w_3(2, 3)
-            w_4(2, 1)
+            w_4(1, ff(1))
+            w_4(2, ff(1))
+            w_1(1, ff(3))
+            w_1(2, ff(3))
 
         @pl.when(j == 2)
         def _():
-            w_4(1, 2)
-            w_4(2, 2)
+            w_4(1, ff(2))
+            w_4(2, ff(2))
 
         @pl.when(j == 3)
         def _():
-            w_4(1, 3)
-            w_4(2, 3)
+            w_4(1, ff(3))
+            w_4(2, ff(3))
 
         def units(u, total):
             pre = dot(N2[...], WB[g, :, col(u)]) + BP[g, pl.ds(1, 1), col(u)]
@@ -645,15 +634,27 @@
 
         lax.fori_loop(0, U // CB, units, 0)
 
-        @pl.when(j == 0)
-        def _():
-            w_2(2, 1)
+        @pl.when(j == 1)
+        def _():
+            w_3(1, ff(2))
+            w_3(2, ff(2))
 
         @pl.when(j >= 1)
         def _():
-            gp = order(j - 1)
-            g_a(1, gp)
-            g_a(2, gp)
+            g_a(1, ff(j - 1))
+            g_a(2, ff(j - 1))
+
+        @pl.when(j == 2)
+        def _():
+            w_3(1, ff(3))
+            w_3(2, ff(3))
+            g_b(1, ff(0))
+            g_b(2, ff(0))
+
+        @pl.when(j == 3)
+        def _():
+            g_z(1, ff(0))
+            g_z(2, ff(0))
 
         def outs(n, _):
             UN[:, col(n)] += dot(ACT[...], WC[g, :, col(n)])
@@ -662,11 +663,15 @@
 
         lax.fori_loop(0, D // CB, outs, 0)
 
-        @pl.when(j >= 2)
-        def _():
-            gp = order(j - 2)
-            g_b(1, gp)
-            g_b(2, gp)
+        @pl.when(j == 0)
+        def _():
+            w_2(1, ff(2))
+            w_2(2, ff(2))
+
+        @pl.when(j == 1)
+        def _():
+            w_2(1, ff(3))
+            w_2(2, ff(3))
 
         def grads(n, _):
             WC[g, col(n), :] = dot(ACTT[col(n), :], cot_ref[...]).astype(BF)
@@ -677,15 +682,11 @@
         g_core(1, g)
         g_core(2, g)
 
-        @pl.when(j >= 3)
-        def _():
-            gp = order(j - 3)
-            g_z(1, gp)
-            g_z(2, gp)
-
         return 0
 
     lax.fori_loop(0, NT, p3, 0)
+    g_b(1, ff(1))
+    g_b(2, ff(1))
 
     VS[...] = jnp.zeros_like(VS)
 
@@ -710,8 +711,8 @@
         return 0
 
     lax.fori_loop(0, T // RB_, p4, 0)
-    g_a(1, order(3))
-    g_a(2, order(3))
+    g_a(1, ff(3))
+    g_a(2, ff(3))
 
     tail_row = iota((16, T), 0)
 
@@ -741,12 +742,10 @@
         return 0
 
     lax.fori_loop(0, NT, p5a, 0)
-    g_b(1, order(2))
-    g_b(2, order(2))
-    g_z(1, order(1))
-    g_z(2, order(1))
-
-    def chain_back(g):
+    g_z(1, ff(1))
+    g_z(2, ff(1))
+
+    def chain_back(g, _):
         @pl.when(z < NT - 1)
         def _():
             chain_wait(GR, g, 1)
@@ -759,11 +758,16 @@
         def _():
             rcopy(SQ.at[g], GR.at[g], c_s.at[1, g], c_r.at[1, g], (dp, z - 1)).start()
 
+        return 0
+
+    lax.fori_loop(0, NT, chain_back, 0)
+    g_b(1, ff(2))
+    g_b(2, ff(2))
     GN1 = UN
     GN1[...] = jnp.zeros_like(GN1)
 
-    def p5b(g, _):
-        chain_back(g)
+    def p5b(t, _):
+        g = last(t)
         gql = []
         gkl = []
         for h in range(HPG):
@@ -818,6 +822,29 @@
 
             gql.append(back(qf, gq))
             gkl.append(back(kf, gk))
+
+        @pl.when(t >= 1)
+        def _():
+            g_a(0, last(t - 1))
+
+        @pl.when(t == 1)
+        def _():
+            g_b(1, ff(3))
+            g_b(2, ff(3))
+
+        @pl.when(t == 2)
+        def _():
+            g_z(1, ff(3))
+            g_z(2, ff(3))
+
+        @pl.when(t >= 2)
+        def _():
+            g_b(0, last(t - 2))
+
+        @pl.when(t == 3)
+        def _():
+            g_z(0, last(0))
+
         comp = None
         for which, parts in ((0, gql), (1, gkl)):
             glog = jnp.concatenate(parts, axis=0)
@@ -842,36 +869,14 @@
         WA[g, pl.ds(D + 32, 16), :] = vec.astype(BF)
         g_core(0, g)
 
-        @pl.when(g == 0)
-        def _():
-            g_b(1, order(3))
-            g_b(2, order(3))
-            g_z(1, order(2))
-            g_z(2, order(2))
-
-        @pl.when(g == 1)
-        def _():
-            g_z(1, order(3))
-            g_z(2, order(3))
-
-        @pl.when(g >= 1)
-        def _():
-            g_a(0, g - 1)
-
-        @pl.when(g >= 2)
-        def _():
-            g_b(0, g - 2)
-
-        @pl.when(g >= 3)
-        def _():
-            g_z(0, g - 3)
-            g_sum(1)
-            g_sum(2)
+        @pl.when(t == 0)
+        def _():
+            g_z(1, ff(2))
+            g_z(2, ff(2))
 
         return 0
 
     lax.fori_loop(0, NT, p5b, 0)
-    g_a(0, NT - 1)
 
     LS[...] = jnp.zeros_like(LS)
 
@@ -891,29 +896,42 @@
 
     partners = [dp + d_core, dp + d_x, dp + d_y] + [high(i) for i in range(nh)]
 
-    def small_sum(i):
-        copy = rcopy(LS.at[i], LR.at[i], l_s.at[i], l_r.at[i], (partners[i], z))
-        copy.start()
-        copy.wait()
+    steps = len(partners)
+
+    def small_start(i):
+        rcopy(LS.at[i], LR.at[i], l_s.at[i], l_r.at[i], (partners[i], z)).start()
+
+    def small_end(i):
+        rcopy(LS.at[i], LR.at[i], l_s.at[i], l_r.at[i], (partners[i], z)).wait()
         LS[i + 1] = LS[i] + LR[i]
 
-    g_b(0, NT - 2)
-    g_z(0, NT - 3)
+    small_start(0)
+    g_a(0, last(3))
+    g_b(0, last(2))
+    small_end(0)
+    small_start(1)
+    g_z(0, last(1))
+    g_sum(1)
+    g_sum(2)
+    small_end(1)
+    small_start(2)
+    g_b(0, last(3))
+    g_z(0, last(2))
+    small_end(2)
+    for i in range(3, steps):
+        small_start(i)
+        small_end(i)
+    LZ[z] = LS[steps]
+    for o in range(1, NT):
+        rcopy(LS.at[steps], LZ.at[z], lz_s.at[o - 1], lz_r.at[z], (dp, lax.rem(z + o, NT))).start()
     o_2(1)
     o_2(2)
-    for i in range(len(partners)):
-        small_sum(i)
-    last = len(partners)
-    g_b(0, NT - 1)
-    g_z(0, NT - 2)
+    g_z(0, last(3))
+    g_sum(0)
     o_3(1)
     o_3(2)
-    LZ[z] = LS[last]
-    for o in range(1, NT):
-        rcopy(LS.at[last], LZ.at[z], lz_s.at[o - 1], lz_r.at[z], (dp, lax.rem(z + o, NT))).start()
-    g_z(0, NT - 1)
+    o_2(0)
     outs = [o_4(1, ob_ref, own_s.at[0]), o_4(2, oc_ref, own_s.at[1])]
-    g_sum(0)
     for o in range(1, NT):
         zz = lax.rem(z + o, NT)
         rcopy(LZ.at[zz], LZ.at[zz], lz_s.at[o - 1], lz_r.at[zz], (dp, z)).wait_recv()
@@ -921,14 +939,13 @@
     for zz in range(1, NT):
         total = total + LZ[zz]
     ov_ref[...] = total
-    o_2(0)
     o_3(0)
     outs.append(o_4(0, oa_ref, own_s.at[2]))
     for copy in outs:
         copy.wait()
 
     for o in range(1, NT):
-        rcopy(LS.at[last], LZ.at[z], lz_s.at[o - 1], lz_r.at[z], (dp, lax.rem(z + o, NT))).wait_send()
+        rcopy(LS.at[steps], LZ.at[z], lz_s.at[o - 1], lz_r.at[z], (dp, lax.rem(z + o, NT))).wait_send()
     small_done()
     for k in range(KINDS):
         w_z_done(k)
@@ -956,8 +973,8 @@
         vm((NT, 8, D), F32),
     ]
     scratch += [vm((NT, 4 * r, D)) for r in R_G]
+    scratch += [vm((NT, r, D)) for r in R_G]
     scratch += [vm((NT, 2, r, D)) for r in R_G]
-    scratch += [vm((NT, r, D)) for r in R_G]
     scratch += [vm((NT, r, D)) for r in R_G]
     scratch += [vm((rows, D)) for rows in ROWS_G]
     scratch += [vm((nhb, r if nh else 16, D)) for r in R_G]
@@ -995,14 +1012,14 @@
         dma((5,)),
         dma((2, NT - 1)),
         dma((2, NT)),
-        dma((KINDS, NT - 1)),
-        dma((4, KINDS, NT)),
+        dma((KINDS, NT)),
         dma((5, KINDS, NT)),
+        dma((6, KINDS, NT)),
+        dma((6, KINDS, NT)),
         dma((5, KINDS, NT)),
-        dma((4, KINDS, NT)),
         dma((KINDS, NT)),
-        dma((4, KINDS)),
-        dma((4, KINDS)),
+        dma((5, KINDS)),
+        dma((5, KINDS)),
         dma((nhb, KINDS)),
         dma((nhb, KINDS)),
         dma((nst,)),

time: 262 us -> 250 us (0.954); the launches traced: 257 us -> 249 us
  Pallas kernels: 228 us -> 219 us
    pallas_call x1, Pallas kernels: 228 us -> 219 us  [layer_call(): pl.pallas_call(functools.partial(layer_kernel, nh), out_shape=(jax.ShapeD...]
where the time goes in v2:
time: 250 us; the launch traced here: 249 us
  Pallas kernels  219 us (88%)
  local copies, waits for them, and re-layouts  16.7 us (7%)
  other arithmetic  11.7 us (5%)
    pallas_call x1, Pallas kernels, layer_call(): pl.pallas_call(functools.partial(layer_kernel, nh), out_shape=(jax.ShapeD...  219 us
    reshape x6, local copies, waits for them, and re-layouts, row(): return v.reshape(1, D)  7.6 us

profile of v2, /device:TPU:1, one launch (start us, length us, event | category | flops | bytes accessed | tf_op | source)
XLA Modules:
  0.0 248.5 jit_solution(4169688260069110127)
XLA Ops:
  0.7 0.1 pad.7.clone
  0.7 0.8 reshape.85
  1.5 1.3 reshape.76.ln1g_ref
  2.8 1.3 reshape.77.ln1b_ref
  4.0 1.3 reshape.78.bout_ref
  5.3 1.3 reshape.79.ln2g_ref
  6.6 1.3 reshape.80.ln2b_ref
  7.8 0.7 reshape.86
  8.5 1.3 reshape.81.bproj_ref
  9.8 0.7 fusion.bp_own
  10.5 0.9 copy.38
  11.4 0.9 copy.39
  12.3 0.7 pad_maximum_fusion.1.ft_own
  13.0 2.4 pad_maximum_fusion.a_own
  15.3 219.4 %shard_map.288 = (bf16[512,768]{1,0:T(8,128)(2,1)}, bf16[512,768]{1,0:T(8,128)(2,1)}, bf16[896,768]{1,0:T(8,128)(2,1)}, bf16[768,768]{1,0:T(8,128)(2,1)}, bf16[768,768]{1,0:T(8,128)(2,1)}, /*index=5*/f32[8,768]{1,0:T(8,128)}) custom-call(s32[1,2]{1,0:T(1,128)} %seq_ref.1, bf16[512,768]{1,0:T(8,128)(2,1)} %x_ref.1, bf16[512,768]{1,0:T(8,128)(2,1)} %cot_ref.1, ...), custom_call_target="tpu_custom_call" | custom-call | tf_op jit(solution)/shard_map/pallas_call | solution.py:1034
  234.7 0.0 copy-start.2
  234.7 0.8 slice_convert_fusion.2
  235.6 1.5 slice_reduce_fusion
  237.1 0.7 reshape_squeeze.3
  237.8 0.8 slice_convert_fusion.1
  238.6 0.7 fusion.1
  239.4 1.8 slice_convert_fusion
  241.2 0.0 copy-done.2
  241.2 0.1 slice.44
  241.3 1.4 convert_bitcast_fusion
  242.6 0.4 copy-done.1
  243.0 1.6 convert_element_type.45
  244.6 0.1 copy-done
  244.6 1.6 convert_element_type.46
  246.2 0.9 copy.43
  247.1 0.5 copy-done.3
  247.6 0.9 copy.44
  (9 shorter events, 0.1 us)
Async XLA Ops:
  234.7 6.5 %copy-start.2 = (bf16[896,768]{1,0:T(8,128)(2,1)S(1)}, bf16[896,768]{1,0:T(8,128)(2,1)}, u32[]{:S(2)}) copy-start(bf16[896,768]{1,0:T(8,128)(2,1)} %get-tuple-element.25) | copy-start | bytes 4128772
  241.2 1.7 copy-start.1
  243.0 1.7 copy-start
  244.6 1.6 copy-start.4
  246.2 1.4 copy-start.3

commit v3 on v2

--- a/solution.py
+++ b/solution.py
@@ -176,14 +176,26 @@
     O = (OA, OB, OC)
     RH = (RHA, RHB, RHC)
 
-    def flip(j):
-        return lax.rem(z // 2 + j // 2, 2) * 2 + lax.rem(z + j, 2)
+    near = z + 1 - 2 * lax.rem(z, 2)
+    mid = 2 - z // 2
+    far = 3 * (1 - z // 2)
+    is_outer = jnp.logical_or(z == 0, z == NT - 1)
+    is_inner = jnp.logical_and(z > 0, z < NT - 1)
+
+    def choose(j, groups):
+        out = groups[-1]
+        for i in range(NT - 2, -1, -1):
+            out = jnp.where(j == i, groups[i], out)
+        return out
+
+    def wo(j):
+        return choose(j, (z, near, mid, far))
 
     def ff(j):
-        return flip(lax.rem(NT - j, NT))
+        return choose(j, (z, far, mid, near))
 
     def last(t):
-        return flip(NT - 1 - t)
+        return choose(t, (far, mid, near, z))
 
     def high(i):
         step = 8 * 2**i
@@ -218,10 +230,19 @@
     def whalf(k, g, s, h):
         return W[k].at[g, pl.ds(mo(s * R_W + h * HALF_W[0], 16), HALF_W[h]), :]
 
-    def w_z(k, g):
-        rcopy(
-            OWN[k].at[pl.ds(mo(slot * R_W, R_W), R_W), :], wrows(k, z, slot), wz_s.at[k, g], w_r.at[0, k, z], (dp, g)
-        ).start()
+    def z_next(g):
+        return jnp.where(g < z, z + 1, z - 1)
+
+    def w_z(k):
+        src = OWN[k].at[pl.ds(mo(slot * R_W, R_W), R_W), :]
+
+        @pl.when(z < NT - 1)
+        def _():
+            rcopy(src, wrows(k, z, slot), wz_s.at[k, 0], w_r.at[0, k, z], (dp, z + 1)).start()
+
+        @pl.when(z > 0)
+        def _():
+            rcopy(src, wrows(k, z, slot), wz_s.at[k, 1], w_r.at[0, k, z], (dp, z - 1)).start()
 
     def w_wait(k, g, stage, ref):
         rcopy(ref, ref, w_s.at[0, k, g], w_r.at[stage, k, g], dev_c).wait_recv()
@@ -229,9 +250,16 @@
     def w_send(k, g, s_stage, r_stage, ref, dev):
         rcopy(ref, ref, w_s.at[s_stage, k, g], w_r.at[r_stage, k, g], dev).start()
 
+    def w_0(k, g):
+        mine = wrows(k, g, slot)
+        w_wait(k, g, 0, mine)
+
+        @pl.when(is_inner)
+        def _():
+            w_send(k, g, 5, 0, mine, (dp, z_next(g)))
+
     def w_1(k, g):
         mine = wrows(k, g, slot)
-        w_wait(k, g, 0, mine)
         w_send(k, g, 0, 1, mine, dev_x)
         w_send(k, g, 1, 2, mine, dev_y)
 
@@ -252,11 +280,21 @@
         for st, ref in enumerate(sent):
             rcopy(ref, ref, w_s.at[st, k, g], w_r.at[0, k, g], dev_c).wait_send()
 
+        @pl.when(is_inner)
+        def _():
+            mine = wrows(k, g, slot)
+            rcopy(mine, mine, w_s.at[5, k, g], w_r.at[0, k, g], dev_c).wait_send()
+
     def w_z_done(k):
-        one = OWN[k].at[pl.ds(mo(slot * R_W, R_W), R_W), :]
-        for i in range(1, NT):
-            g = flip(i)
-            rcopy(one, wrows(k, z, slot), wz_s.at[k, g], w_r.at[0, k, z], (dp, g)).wait_send()
+        src = OWN[k].at[pl.ds(mo(slot * R_W, R_W), R_W), :]
+
+        @pl.when(z < NT - 1)
+        def _():
+            rcopy(src, wrows(k, z, slot), wz_s.at[k, 0], w_r.at[0, k, z], (dp, z + 1)).wait_send()
+
+        @pl.when(z > 0)
+        def _():
+            rcopy(src, wrows(k, z, slot), wz_s.at[k, 1], w_r.at[0, k, z], (dp, z - 1)).wait_send()
 
     small = ((ft_own, FT), (bp_own, BP))
 
@@ -282,13 +320,9 @@
         pltpu.make_async_copy(c_own, WC.at[z], own_s.at[4]),
     ]
     small_send()
-    for i in range(1, NT):
-        w_z(0, flip(i))
+    w_z(0)
     for copy in local:
         copy.start()
-    for j in range(1, NT):
-        w_z(1, ff(j))
-        w_z(2, ff(j))
 
     def grows(k, g, s, n=1):
         return W[k].at[g, pl.ds(mo(s * R_G[k], 16), n * R_G[k]), :]
@@ -332,14 +366,36 @@
         add_rows(W[k].at[g], slot_x * R_G[k] + HALF_G[k][0], ra(k, g, 1), HALF_G[k][1])
         g_send(k, g, 3, grows(k, g, slot_x), RB[k].at[g, 0], dev_x)
 
-    def g_z(k, g):
+    def g_y(k, g):
         for i in range(2):
             g_wait(k, g, 3 + i, RB[k].at[g, i])
             add_rows(W[k].at[g], slot * R_G[k], RB[k].at[g, i], R_G[k])
 
-        @pl.when(g != z)
-        def _():
-            rcopy(grows(k, g, slot), ZR[k].at[z], g_s.at[5, k, g], z_r.at[k, z], (dp, g)).start()
+    def z_send(k, g):
+        @pl.when(z < g)
+        def _():
+            rcopy(grows(k, g, slot), ZR[k].at[g], g_s.at[5, k, g], z_r.at[k, g], (dp, z + 1)).start()
+
+        @pl.when(z > g)
+        def _():
+            at = jnp.where(z - 1 == g, NT, g)
+            rcopy(grows(k, g, slot), ZR[k].at[at], g_s.at[5, k, g], z_r.at[k, at], (dp, z - 1)).start()
+
+    def z_add(k, g, at):
+        ref = ZR[k].at[at]
+        rcopy(ref, ref, g_s.at[0, k, 0], z_r.at[k, at], dev_c).wait_recv()
+        add_rows(W[k].at[g], slot * R_G[k], ref, R_G[k])
+
+    def z_out(k, g):
+        @pl.when(is_outer)
+        def _():
+            z_send(k, g)
+
+    def z_in(k, g):
+        @pl.when(is_inner)
+        def _():
+            z_add(k, g, g)
+            z_send(k, g)
 
     def g_done(k, g):
         one = grows(k, g, 0)
@@ -364,22 +420,15 @@
         rcopy(ref, ref, o_s.at[stage, k], o_r.at[stage, k], dev).start()
 
     def g_sum(k):
-        for o in range(1, NT):
-            zz = lax.rem(z + o, NT)
-            ref = ZR[k].at[zz]
-            rcopy(ref, ref, g_s.at[0, k, 0], z_r.at[k, zz], (dp, z)).wait_recv()
-        blk = 16
-
-        def body(i, _):
-            at = pl.ds(mo(i * blk, 16), blk)
-            mine = pl.ds(mo(slot * R_G[k] + i * blk, 16), blk)
-            acc = W[k][z, mine, :].astype(F32)
-            for o in range(1, NT):
-                acc = acc + ZR[k][lax.rem(z + o, NT), at, :].astype(F32)
-            O[k][mine, :] = acc.astype(BF)
-            return 0
-
-        lax.fori_loop(0, R_G[k] // blk, body, 0)
+        @pl.when(z > 0)
+        def _():
+            z_add(k, z, z)
+
+        @pl.when(z < NT - 1)
+        def _():
+            z_add(k, z, NT)
+
+        O[k][pl.ds(mo(slot * R_G[k], 16), R_G[k]), :] = W[k][z, pl.ds(mo(slot * R_G[k], 16), R_G[k]), :]
         for i in range(nh):
             rcopy(orows(k, slot), RH[k].at[i], h_s.at[i, k], h_r.at[i, k], (high(i), z)).start()
             rcopy(orows(k, slot), RH[k].at[i], h_s.at[i, k], h_r.at[i, k], (high(i), z)).wait()
@@ -460,32 +509,49 @@
     for copy in local[:3]:
         copy.wait()
 
+    def chain_wait(buf, g, stage):
+        rcopy(buf.at[g], buf.at[g], c_s.at[stage, g], c_r.at[stage, g], (dp, z)).wait_recv()
+
+    def chain_send(g):
+        rcopy(SQ.at[g], CR.at[g], c_s.at[0, g], c_r.at[0, g], (dp, z + 1)).start()
+
     def p1(j, _):
-        g = flip(j)
+        g = wo(j)
 
         @pl.when(j == 1)
         def _():
-            small_wait(flip(1))
-            w_1(0, flip(1))
-            w_2(0, flip(1))
-            w_1(0, flip(2))
-            w_1(0, flip(3))
-            w_3(0, flip(1))
-            w_2(0, flip(2))
-            w_4(0, flip(1))
+            small_wait(near)
+            w_0(0, near)
+            w_1(0, near)
+            w_z(1)
+            w_0(0, mid)
+            w_1(0, mid)
+            w_z(2)
+            w_2(0, near)
+            w_3(0, near)
+            w_0(0, far)
+            w_1(0, far)
+            w_2(0, mid)
+            w_4(0, near)
+            w_0(1, near)
 
         @pl.when(j == 2)
         def _():
-            small_wait(flip(2))
-            w_2(0, flip(3))
-            w_3(0, flip(2))
-            w_4(0, flip(2))
+            small_wait(mid)
+            w_3(0, mid)
+            w_0(2, near)
+            w_2(0, far)
+            w_4(0, mid)
 
         @pl.when(j == 3)
         def _():
-            small_wait(flip(3))
-            w_3(0, flip(3))
-            w_4(0, flip(3))
+            small_wait(far)
+            w_0(1, mid)
+            w_3(0, far)
+            w_1(1, near)
+            w_1(2, near)
+            w_0(2, mid)
+            w_4(0, far)
 
         bias = jnp.transpose(BP[g])[:QKV, 0:1]
         qkv = (dot(WA[g, pl.ds(0, QKV), :], N1[...], 1, 1) + bias).astype(BF)
@@ -519,37 +585,39 @@
         def _():
             for h in range(HPG):
                 SQ[g, h] = ST[g * HPG + h].astype(BF)
-            rcopy(SQ.at[g], CR.at[g], c_s.at[0, g], c_r.at[0, g], (dp, z + 1)).start()
+            chain_send(g)
+
+        for zz, jj, ready in ((1, 1, (0, 1)), (1, 2, (2,)), (1, 3, (3,)), (2, 2, (1,)), (2, 3, (0, 2, 3))):
+
+            @pl.when(jnp.logical_and(z == zz, j == jj))
+            def _():
+                for gg in ready:
+                    chain_wait(CR, gg, 0)
+                    for h in range(HPG):
+                        hh = gg * HPG + h
+                        carried = jnp.where(from_prev, CR[gg, h].astype(F32), 0.0)
+                        SQ[gg, h] = (ST[hh] + carried).astype(BF)
+                    chain_send(gg)
 
         return 0
 
     lax.fori_loop(0, NT, p1, 0)
-    w_1(1, ff(1))
-    w_1(2, ff(1))
-
-    def chain_wait(buf, g, stage):
-        rcopy(buf.at[g], buf.at[g], c_s.at[stage, g], c_r.at[stage, g], (dp, z)).wait_recv()
+    for k in (1, 2):
+        w_0(k, far)
+        w_1(k, far)
+    w_2(1, near)
+    w_2(2, near)
 
     def p1b(g, _):
-        @pl.when(z > 0)
+        @pl.when(z == NT - 1)
         def _():
             chain_wait(CR, g, 0)
 
         for h in range(HPG):
             CT[g * HPG + h] = jnp.where(from_prev, CR[g, h], jnp.zeros((AUG, 2 * HD), BF))
-
-        @pl.when(jnp.logical_and(z > 0, z < NT - 1))
-        def _():
-            for h in range(HPG):
-                hh = g * HPG + h
-                SQ[g, h] = (ST[hh] + CT[hh].astype(F32)).astype(BF)
-            rcopy(SQ.at[g], CR.at[g], c_s.at[0, g], c_r.at[0, g], (dp, z + 1)).start()
-
         return 0
 
     lax.fori_loop(0, NT, p1b, 0)
-    w_2(1, ff(1))
-    w_2(2, ff(1))
 
     def p1c(g, _):
         for h in range(HPG):
@@ -561,6 +629,11 @@
         return 0
 
     lax.fori_loop(0, NT, p1c, 0)
+    for k in (1, 2):
+        w_1(k, mid)
+    for k in (1, 2):
+        w_3(k, near)
+        w_2(k, far)
 
     def p2(n, _):
         acc = None
@@ -581,10 +654,8 @@
         return 0
 
     lax.fori_loop(0, T // 128, p2b, 0)
-    w_3(1, ff(1))
-    w_3(2, ff(1))
-    w_1(1, ff(2))
-    w_1(2, ff(2))
+    w_3(1, far)
+    w_3(2, far)
 
     @pl.when(z < NT - 1)
     def _():
@@ -601,22 +672,10 @@
     def p3(j, _):
         g = ff(j)
 
-        @pl.when(j == 1)
-        def _():
-            w_4(1, ff(1))
-            w_4(2, ff(1))
-            w_1(1, ff(3))
-            w_1(2, ff(3))
-
-        @pl.when(j == 2)
-        def _():
-            w_4(1, ff(2))
-            w_4(2, ff(2))
-
-        @pl.when(j == 3)
-        def _():
-            w_4(1, ff(3))
-            w_4(2, ff(3))
+        @pl.when(j > 0)
+        def _():
+            w_4(1, g)
+            w_4(2, g)
 
         def units(u, total):
             pre = dot(N2[...], WB[g, :, col(u)]) + BP[g, pl.ds(1, 1), col(u)]
@@ -634,27 +693,20 @@
 
         lax.fori_loop(0, U // CB, units, 0)
 
-        @pl.when(j == 1)
-        def _():
-            w_3(1, ff(2))
-            w_3(2, ff(2))
-
         @pl.when(j >= 1)
         def _():
             g_a(1, ff(j - 1))
             g_a(2, ff(j - 1))
 
+        @pl.when(j == 1)
+        def _():
+            w_3(1, mid)
+            w_3(2, mid)
+
         @pl.when(j == 2)
         def _():
-            w_3(1, ff(3))
-            w_3(2, ff(3))
-            g_b(1, ff(0))
-            g_b(2, ff(0))
-
-        @pl.when(j == 3)
-        def _():
-            g_z(1, ff(0))
-            g_z(2, ff(0))
+            g_b(1, z)
+            g_b(2, z)
 
         def outs(n, _):
             UN[:, col(n)] += dot(ACT[...], WC[g, :, col(n)])
@@ -665,13 +717,8 @@
 
         @pl.when(j == 0)
         def _():
-            w_2(1, ff(2))
-            w_2(2, ff(2))
-
-        @pl.when(j == 1)
-        def _():
-            w_2(1, ff(3))
-            w_2(2, ff(3))
+            w_2(1, mid)
+            w_2(2, mid)
 
         def grads(n, _):
             WC[g, col(n), :] = dot(ACTT[col(n), :], cot_ref[...]).astype(BF)
@@ -685,8 +732,8 @@
         return 0
 
     lax.fori_loop(0, NT, p3, 0)
-    g_b(1, ff(1))
-    g_b(2, ff(1))
+    g_b(1, far)
+    g_b(2, far)
 
     VS[...] = jnp.zeros_like(VS)
 
@@ -711,8 +758,8 @@
         return 0
 
     lax.fori_loop(0, T // RB_, p4, 0)
-    g_a(1, ff(3))
-    g_a(2, ff(3))
+    g_a(1, near)
+    g_a(2, near)
 
     tail_row = iota((16, T), 0)
 
@@ -742,8 +789,6 @@
         return 0
 
     lax.fori_loop(0, NT, p5a, 0)
-    g_z(1, ff(1))
-    g_z(2, ff(1))
 
     def chain_back(g, _):
         @pl.when(z < NT - 1)
@@ -760,11 +805,21 @@
 
         return 0
 
-    lax.fori_loop(0, NT, chain_back, 0)
-    g_b(1, ff(2))
-    g_b(2, ff(2))
     GN1 = UN
     GN1[...] = jnp.zeros_like(GN1)
+
+    def back(feat, grads):
+        out = []
+        for b in range(NB):
+            bs = slice(b * CB, (b + 1) * CB)
+            p = feat[:HD, bs].astype(F32)
+            m = feat[HD:, bs].astype(F32)
+            g1 = grads[b][:HD]
+            g2 = grads[b][HD:]
+            s1 = jnp.sum(g1 * p, axis=0, keepdims=True)
+            s2 = jnp.sum(g2 * m, axis=0, keepdims=True)
+            out.append((p * (g1 - s1) - m * (g2 - s2)).astype(BF))
+        return jnp.concatenate(out, axis=1)
 
     def p5b(t, _):
         g = last(t)
@@ -779,8 +834,6 @@
             kn = kf.T
             vn = va.T
             ctt = CT[hh].T
-            gkc = jnp.where(from_next, GR[g, h], jnp.zeros((AUG, 2 * HD), BF))
-            gkt = gkc.T
             gq = [None] * NB
             gk = [None] * NB
             gv = [None] * NB
@@ -803,47 +856,60 @@
                     gv[ki] = pv if gv[ki] is None else gv[ki] + pv
             for ki in range(NB):
                 ks = slice(ki * CB, (ki + 1) * CB)
-                gk[ki] = gk[ki] + dot(gkt, va[:, ks])
-                gv[ki] = gv[ki] + dot(gkc[:HD], kf[:, ks])
-                GQ[pl.ds(2 * HC + h * HD, HD), ks] = gv[ki].astype(BF)
-
-            def back(feat, grads):
-                out = []
-                for b in range(NB):
-                    bs = slice(b * CB, (b + 1) * CB)
-                    p = feat[:HD, bs].astype(F32)
-                    m = feat[HD:, bs].astype(F32)
-                    g1 = grads[b][:HD]
-                    g2 = grads[b][HD:]
-                    s1 = jnp.sum(g1 * p, axis=0, keepdims=True)
-                    s2 = jnp.sum(g2 * m, axis=0, keepdims=True)
-                    out.append((p * (g1 - s1) - m * (g2 - s2)).astype(BF))
-                return jnp.concatenate(out, axis=1)
-
+                NM[3 * h, :HD, ks] = gk[ki][:HD]
+                NM[3 * h + 1, :HD, ks] = gk[ki][HD:]
+                NM[3 * h + 2, :HD, ks] = gv[ki]
             gql.append(back(qf, gq))
+
+        @pl.when(t == 0)
+        def _():
+            lax.fori_loop(0, NT, chain_back, 0)
+            for k in (1, 2):
+                g_b(k, mid)
+                g_y(k, z)
+                g_y(k, far)
+
+        @pl.when(t >= 1)
+        def _():
+            g_a(0, last(t - 1))
+
+        @pl.when(t == 1)
+        def _():
+            g_b(1, near)
+            g_b(2, near)
+
+        @pl.when(t >= 2)
+        def _():
+            g_b(0, last(t - 2))
+
+        for k in (1, 2):
+
+            @pl.when(t == 2)
+            def _():
+                z_in(k, far)
+
+            @pl.when(t == 3)
+            def _():
+                z_in(k, mid)
+
+        @pl.when(t == 3)
+        def _():
+            g_y(0, far)
+            z_out(0, far)
+
+        for h in range(HPG):
+            hh = g * HPG + h
+            kf = KF[hh]
+            va = VA[hh]
+            gkc = jnp.where(from_next, GR[g, h], jnp.zeros((AUG, 2 * HD), BF))
+            gkt = gkc.T
+            gk = [None] * NB
+            for ki in range(NB):
+                ks = slice(ki * CB, (ki + 1) * CB)
+                gk[ki] = jnp.concatenate([NM[3 * h, :HD, ks], NM[3 * h + 1, :HD, ks]], axis=0) + dot(gkt, va[:, ks])
+                gv = NM[3 * h + 2, :HD, ks] + dot(gkc[:HD], kf[:, ks])
+                GQ[pl.ds(2 * HC + h * HD, HD), ks] = gv.astype(BF)
             gkl.append(back(kf, gk))
-
-        @pl.when(t >= 1)
-        def _():
-            g_a(0, last(t - 1))
-
-        @pl.when(t == 1)
-        def _():
-            g_b(1, ff(3))
-            g_b(2, ff(3))
-
-        @pl.when(t == 2)
-        def _():
-            g_z(1, ff(3))
-            g_z(2, ff(3))
-
-        @pl.when(t >= 2)
-        def _():
-            g_b(0, last(t - 2))
-
-        @pl.when(t == 3)
-        def _():
-            g_z(0, last(0))
 
         comp = None
         for which, parts in ((0, gql), (1, gkl)):
@@ -869,10 +935,25 @@
         WA[g, pl.ds(D + 32, 16), :] = vec.astype(BF)
         g_core(0, g)
 
-        @pl.when(t == 0)
-        def _():
-            g_z(1, ff(2))
-            g_z(2, ff(2))
+        for k in (1, 2):
+
+            @pl.when(t == 0)
+            def _():
+                z_out(k, far)
+
+            @pl.when(t == 1)
+            def _():
+                g_y(k, mid)
+                z_out(k, mid)
+
+            @pl.when(t == 2)
+            def _():
+                g_y(k, near)
+                z_out(k, near)
+
+            @pl.when(t == 3)
+            def _():
+                z_in(k, near)
 
         return 0
 
@@ -906,17 +987,22 @@
         LS[i + 1] = LS[i] + LR[i]
 
     small_start(0)
-    g_a(0, last(3))
-    g_b(0, last(2))
+    g_a(0, z)
+    g_b(0, near)
+    g_y(0, mid)
+    z_out(0, mid)
+    z_in(0, far)
     small_end(0)
     small_start(1)
-    g_z(0, last(1))
+    g_b(0, z)
+    z_in(0, mid)
+    g_y(0, near)
+    z_out(0, near)
+    z_in(0, near)
+    small_end(1)
+    small_start(2)
     g_sum(1)
     g_sum(2)
-    small_end(1)
-    small_start(2)
-    g_b(0, last(3))
-    g_z(0, last(2))
     small_end(2)
     for i in range(3, steps):
         small_start(i)
@@ -926,7 +1012,7 @@
         rcopy(LS.at[steps], LZ.at[z], lz_s.at[o - 1], lz_r.at[z], (dp, lax.rem(z + o, NT))).start()
     o_2(1)
     o_2(2)
-    g_z(0, last(3))
+    g_y(0, z)
     g_sum(0)
     o_3(1)
     o_3(2)
@@ -975,7 +1061,7 @@
     scratch += [vm((NT, 4 * r, D)) for r in R_G]
     scratch += [vm((NT, r, D)) for r in R_G]
     scratch += [vm((NT, 2, r, D)) for r in R_G]
-    scratch += [vm((NT, r, D)) for r in R_G]
+    scratch += [vm((NT + 1, r, D)) for r in R_G]
     scratch += [vm((rows, D)) for rows in ROWS_G]
     scratch += [vm((nhb, r if nh else 16, D)) for r in R_G]
     scratch += [vm((nst + 1, 8, D), F32), vm((nst, 8, D), F32), vm((NT, 8, D), F32)]
@@ -1012,12 +1098,12 @@
         dma((5,)),
         dma((2, NT - 1)),
         dma((2, NT)),
-        dma((KINDS, NT)),
-        dma((5, KINDS, NT)),
+        dma((KINDS, 2)),
+        dma((6, KINDS, NT)),
         dma((6, KINDS, NT)),
         dma((6, KINDS, NT)),
         dma((5, KINDS, NT)),
-        dma((KINDS, NT)),
+        dma((KINDS, NT + 1)),
         dma((5, KINDS)),
         dma((5, KINDS)),
         dma((nhb, KINDS)),

time: 250 us -> 226 us (0.904)
  Pallas kernels: 219 us -> 196 us
    pallas_call x1, Pallas kernels: 219 us -> 196 us  [layer_call(): pl.pallas_call(functools.partial(layer_kernel, nh), out_shape=(jax.ShapeD...]
where the time goes in v3:
time: 226 us; the launch traced here: 225 us
  Pallas kernels  196 us (87%)
  local copies, waits for them, and re-layouts  16.7 us (7%)
  other arithmetic  11.7 us (5%)
    pallas_call x1, Pallas kernels, layer_call(): pl.pallas_call(functools.partial(layer_kernel, nh), out_shape=(jax.ShapeD...  196 us
    reshape x6, local copies, waits for them, and re-layouts, row(): return v.reshape(1, D)  7.6 us

profile of v3, /device:TPU:1, one launch (start us, length us, event | category | flops | bytes accessed | tf_op | source)
XLA Modules:
  0.0 224.9 jit_solution(9804476800254062545)
XLA Ops:
  0.7 0.1 pad.7.clone
  0.7 0.8 reshape.85
  1.5 1.3 reshape.76.ln1g_ref
  2.8 1.3 reshape.77.ln1b_ref
  4.0 1.3 reshape.78.bout_ref
  5.3 1.3 reshape.79.ln2g_ref
  6.6 1.3 reshape.80.ln2b_ref
  7.8 0.7 reshape.86
  8.5 1.3 reshape.81.bproj_ref
  9.8 0.7 fusion.bp_own
  10.5 0.9 copy.38
  11.4 0.9 copy.39
  12.3 0.7 pad_maximum_fusion.1.ft_own
  13.0 2.4 %pad_maximum_fusion.a_own = bf16[768,768]{1,0:T(8,128)(2,1)} fusion(bf16[192,768]{1,0:T(8,128)(2,1)} %param.24, bf16[576,768]{1,0:T(8,128)(2,1)} %bitcast.14), kind=kLoop, calls=%fused_computation.1 | loop fusion | flops 2359296 | bytes 2359296 | tf_op jit(solution)/shard_map/concatenate | solution.py:1160
  15.3 195.7 %shard_map.288 = (bf16[512,768]{1,0:T(8,128)(2,1)}, bf16[512,768]{1,0:T(8,128)(2,1)}, bf16[896,768]{1,0:T(8,128)(2,1)}, bf16[768,768]{1,0:T(8,128)(2,1)}, bf16[768,768]{1,0:T(8,128)(2,1)}, /*index=5*/f32[8,768]{1,0:T(8,128)}) custom-call(s32[1,2]{1,0:T(1,128)} %seq_ref.1, bf16[512,768]{1,0:T(8,128)(2,1)} %x_ref.1, bf16[512,768]{1,0:T(8,128)(2,1)} %cot_ref.1, ...), custom_call_target="tpu_custom_call" | custom-call | tf_op jit(solution)/shard_map/pallas_call | solution.py:1120
  211.1 0.8 slice_convert_fusion.2
  212.0 1.5 slice_reduce_fusion
  213.5 0.7 reshape_squeeze.3
  214.1 0.8 slice_convert_fusion.1
  215.0 0.7 fusion.1
  215.7 1.8 slice_convert_fusion
  217.5 0.0 copy-done.2
  217.5 0.1 slice.44
  217.6 1.4 convert_bitcast_fusion
  219.0 0.4 copy-done.1
  219.3 1.6 convert_element_type.45
  220.9 0.1 copy-done
  221.0 1.6 convert_element_type.46
  222.6 0.0 copy-done.4
  222.6 0.9 copy.43
  223.5 0.5 copy-done.3
  224.0 0.9 copy.44
  (9 shorter events, 0.1 us)
Async XLA Ops:
  211.1 6.5 %copy-start.2 = (bf16[896,768]{1,0:T(8,128)(2,1)S(1)}, bf16[896,768]{1,0:T(8,128)(2,1)}, u32[]{:S(2)}) copy-start(bf16[896,768]{1,0:T(8,128)(2,1)} %get-tuple-element.25) | copy-start | bytes 4128772
  217.6 1.7 copy-start.1
  219.3 1.7 copy-start
  221.0 1.6 copy-start.4
  222.6 1.4 copy-start.3

commit v4 on v3

--- a/solution.py
+++ b/solution.py
@@ -65,23 +65,36 @@
     seq_ref,
     x_ref,
     cot_ref,
-    ln1g_ref,
-    ln1b_ref,
-    bout_ref,
-    ln2g_ref,
-    ln2b_ref,
-    bproj_ref,
+    ln1g_in,
+    ln1b_in,
+    bout_in,
+    ln2g_in,
+    ln2b_in,
+    bproj_in,
+    bfc_in,
+    bqkv_in,
+    fq_in,
+    fk_in,
     a_own,
+    a_out,
     b_own,
     c_own,
-    ft_own,
-    bp_own,
     res_ref,
     gin_ref,
     oa_ref,
+    oo_ref,
     ob_ref,
     oc_ref,
-    ov_ref,
+    gfq_ref,
+    gfk_ref,
+    gbqkv_ref,
+    gbfc_ref,
+    gbproj_ref,
+    gbout_ref,
+    gln2g_ref,
+    gln2b_ref,
+    gln1g_ref,
+    gln1b_ref,
     WA,
     WB,
     WC,
@@ -135,6 +148,10 @@
     GC,
     GQ,
     VS,
+    PV,
+    ft_own,
+    bp_own,
+    WO,
     own_s,
     sm_s,
     sm_r,
@@ -213,6 +230,15 @@
     slot_y = core * 4 + (1 - by) * 2 + bx
     slot_d = core * 4 + (1 - by) * 2 + (1 - bx)
 
+    for i, ref in enumerate((ln1g_in, ln1b_in, bout_in, ln2g_in, ln2b_in, bproj_in)):
+        PV[i] = ref[...].reshape(1, D)
+    ln1g_ref, ln1b_ref, bout_ref, ln2g_ref, ln2b_ref, bproj_ref = (PV.at[i] for i in range(6))
+    bp_own[...] = jnp.zeros_like(bp_own)
+    bp_own[0:3, 0:HC] = bqkv_in[...]
+    bp_own[3:4, :] = bfc_in[...].reshape(1, D)
+    for h in range(HPG):
+        ft_own[h * HD : (h + 1) * HD, :] = jnp.concatenate([fq_in[h], fk_in[h]], axis=1)
+
     peers = [(dp + d_core, z), (dp + d_x, z), (dp + d_y, z)]
     peers += [(high(i), z) for i in range(nh)]
     peers += [(dp, lax.rem(z + o, NT)) for o in range(1, NT)]
@@ -233,16 +259,28 @@
     def z_next(g):
         return jnp.where(g < z, z + 1, z - 1)
 
+    def own_rows(k):
+        at = pl.ds(mo(slot * R_W, R_W), R_W)
+        if k:
+            return ((slot >= 0, OWN[k].at[at, :]),)
+        split = QKV // R_W
+        low = jnp.where(slot < split, slot, 0)
+        high = jnp.where(slot < split, 0, slot - split)
+        return (
+            (slot < split, a_own.at[pl.ds(mo(low * R_W, R_W), R_W), :]),
+            (slot >= split, a_out.at[pl.ds(mo(high * R_W, R_W), R_W), :]),
+        )
+
     def w_z(k):
-        src = OWN[k].at[pl.ds(mo(slot * R_W, R_W), R_W), :]
-
-        @pl.when(z < NT - 1)
-        def _():
-            rcopy(src, wrows(k, z, slot), wz_s.at[k, 0], w_r.at[0, k, z], (dp, z + 1)).start()
-
-        @pl.when(z > 0)
-        def _():
-            rcopy(src, wrows(k, z, slot), wz_s.at[k, 1], w_r.at[0, k, z], (dp, z - 1)).start()
+        for here, src in own_rows(k):
+
+            @pl.when(jnp.logical_and(here, z < NT - 1))
+            def _():
+                rcopy(src, wrows(k, z, slot), wz_s.at[k, 0], w_r.at[0, k, z], (dp, z + 1)).start()
+
+            @pl.when(jnp.logical_and(here, z > 0))
+            def _():
+                rcopy(src, wrows(k, z, slot), wz_s.at[k, 1], w_r.at[0, k, z], (dp, z - 1)).start()
 
     def w_wait(k, g, stage, ref):
         rcopy(ref, ref, w_s.at[0, k, g], w_r.at[stage, k, g], dev_c).wait_recv()
@@ -286,7 +324,7 @@
             rcopy(mine, mine, w_s.at[5, k, g], w_r.at[0, k, g], dev_c).wait_send()
 
     def w_z_done(k):
-        src = OWN[k].at[pl.ds(mo(slot * R_W, R_W), R_W), :]
+        src = own_rows(k)[0][1]
 
         @pl.when(z < NT - 1)
         def _():
@@ -315,12 +353,19 @@
     local = [
         pltpu.make_async_copy(ft_own, FT.at[z], own_s.at[0]),
         pltpu.make_async_copy(bp_own, BP.at[z], own_s.at[1]),
-        pltpu.make_async_copy(a_own, WA.at[z, pl.ds(0, D), :], own_s.at[2]),
+        pltpu.make_async_copy(a_own, WA.at[z, pl.ds(0, QKV), :], own_s.at[2]),
+        pltpu.make_async_copy(a_out, WA.at[z, pl.ds(QKV, HC), :], own_s.at[5]),
         pltpu.make_async_copy(b_own, WB.at[z], own_s.at[3]),
         pltpu.make_async_copy(c_own, WC.at[z], own_s.at[4]),
     ]
     small_send()
     w_z(0)
+
+    @pl.when(is_outer)
+    def _():
+        w_z(1)
+        w_z(2)
+
     for copy in local:
         copy.start()
 
@@ -447,14 +492,29 @@
         o_wait(k, 3, ohalf(k, slot_d, 1))
         o_send(k, 4, orows(k, core * 4, 4), dev_c)
 
-    def o_4(k, out, sem):
+    def o_4(k):
         o_wait(k, 4, orows(k, (1 - core) * 4, 4))
-        copy = pltpu.make_async_copy(O[k], out, sem)
-        copy.start()
         sent = [orows(k, slot)] * 2 + [ohalf(k, slot_x, 0), ohalf(k, slot_y, 1), orows(k, core * 4, 4)]
         for st, ref in enumerate(sent):
             rcopy(ref, ref, o_s.at[st, k], o_r.at[0, k], dev_c).wait_send()
+
+    def widen(src, start, dst, first, n):
+        def body(i, _):
+            dst[pl.ds(mo(first + i * 64, 64), 64), :] = src[pl.ds(mo(start + i * 64, 64), 64), :].astype(F32)
+            return 0
+
+        lax.fori_loop(0, n // 64, body, 0)
+
+    def write(src, dst, sem):
+        copy = pltpu.make_async_copy(src, dst, sem)
+        copy.start()
         return copy
+
+    def out_ff(k, big, part, out, sem):
+        widen(O[k], 0, big, 0, T)
+        first = write(big, out.at[pl.ds(0, T), :], own_s.at[sem])
+        widen(O[k], T, GN2, part * (D - T), D - T)
+        return first, write(GN2.at[pl.ds(part * (D - T), D - T), :], out.at[pl.ds(T, D - T), :], own_s.at[sem + 1])
 
     def iota(shape, axis):
         return lax.broadcasted_iota(jnp.int32, shape, axis)
@@ -506,7 +566,7 @@
     def _():
         GR[...] = jnp.zeros_like(GR)
 
-    for copy in local[:3]:
+    for copy in local[:4]:
         copy.wait()
 
     def chain_wait(buf, g, stage):
@@ -515,49 +575,89 @@
     def chain_send(g):
         rcopy(SQ.at[g], CR.at[g], c_s.at[0, g], c_r.at[0, g], (dp, z + 1)).start()
 
+    def chain_pass(g):
+        chain_wait(CR, g, 0)
+        for h in range(HPG):
+            carried = jnp.where(from_prev, CR[g, h].astype(F32), 0.0)
+            SQ[g, h] = (ST[g * HPG + h] + carried).astype(BF)
+        chain_send(g)
+
     def p1(j, _):
         g = wo(j)
 
         @pl.when(j == 1)
         def _():
-            small_wait(near)
             w_0(0, near)
             w_1(0, near)
-            w_z(1)
-            w_0(0, mid)
-            w_1(0, mid)
-            w_z(2)
-            w_2(0, near)
-            w_3(0, near)
-            w_0(0, far)
-            w_1(0, far)
-            w_2(0, mid)
+            small_wait(near)
+
+            @pl.when(is_inner)
+            def _():
+                w_0(0, mid)
+                w_1(0, mid)
+                w_0(1, near)
+                w_2(0, near)
+                w_0(0, far)
+                w_1(0, far)
+                w_0(2, near)
+                w_0(1, far)
+                w_2(0, mid)
+                w_3(0, near)
+
+            @pl.when(is_outer)
+            def _():
+                w_2(0, near)
+                w_0(0, mid)
+                w_1(0, mid)
+                w_3(0, near)
+                w_0(0, far)
+                w_1(0, far)
+
             w_4(0, near)
-            w_0(1, near)
 
         @pl.when(j == 2)
         def _():
             small_wait(mid)
-            w_3(0, mid)
-            w_0(2, near)
-            w_2(0, far)
+
+            @pl.when(is_inner)
+            def _():
+                w_0(2, far)
+                w_z(1)
+                w_z(2)
+                w_2(0, far)
+                w_3(0, mid)
+                w_1(1, far)
+                w_1(2, far)
+
+            @pl.when(is_outer)
+            def _():
+                w_2(0, mid)
+                w_0(1, far)
+                w_2(0, far)
+                w_1(1, far)
+                w_3(0, mid)
+                w_0(2, far)
+                w_1(2, far)
+
             w_4(0, mid)
 
         @pl.when(j == 3)
         def _():
             small_wait(far)
-            w_0(1, mid)
             w_3(0, far)
-            w_1(1, near)
-            w_1(2, near)
-            w_0(2, mid)
+
+            @pl.when(is_inner)
+            def _():
+                w_0(1, mid)
+
             w_4(0, far)
 
-        bias = jnp.transpose(BP[g])[:QKV, 0:1]
+        bias = jnp.transpose(BP[g, :, 0:256])
+        bias = jnp.concatenate([bias[:HC, i : i + 1] for i in range(3)], axis=0)
         qkv = (dot(WA[g, pl.ds(0, QKV), :], N1[...], 1, 1) + bias).astype(BF)
         QK[g] = qkv[: 2 * HC]
-        ql = dot(block_diag(g, 0), qkv[:HC])
-        kl = dot(block_diag(g, 1), qkv[HC : 2 * HC])
+        ql = dot(block_diag(g, 0), qkv[:HC], 0, 0)
+        kl = dot(block_diag(g, 1), qkv[HC : 2 * HC], 0, 0)
         for h in range(HPG):
             hh = g * HPG + h
             rows = slice(h * HD, (h + 1) * HD)
@@ -587,26 +687,62 @@
                 SQ[g, h] = ST[g * HPG + h].astype(BF)
             chain_send(g)
 
-        for zz, jj, ready in ((1, 1, (0, 1)), (1, 2, (2,)), (1, 3, (3,)), (2, 2, (1,)), (2, 3, (0, 2, 3))):
+        for zz, jj, ready in ((1, 1, (0, 1)), (1, 2, (2,)), (2, 2, (1,))):
 
             @pl.when(jnp.logical_and(z == zz, j == jj))
             def _():
                 for gg in ready:
-                    chain_wait(CR, gg, 0)
-                    for h in range(HPG):
-                        hh = gg * HPG + h
-                        carried = jnp.where(from_prev, CR[gg, h].astype(F32), 0.0)
-                        SQ[gg, h] = (ST[hh] + carried).astype(BF)
-                    chain_send(gg)
+                    chain_pass(gg)
 
         return 0
 
     lax.fori_loop(0, NT, p1, 0)
-    for k in (1, 2):
-        w_0(k, far)
-        w_1(k, far)
-    w_2(1, near)
-    w_2(2, near)
+    w_2(1, far)
+
+    @pl.when(z == 1)
+    def _():
+        chain_pass(3)
+
+    @pl.when(z == 2)
+    def _():
+        chain_pass(0)
+        chain_pass(2)
+
+    @pl.when(is_inner)
+    def _():
+        w_0(2, mid)
+
+    @pl.when(is_outer)
+    def _():
+        w_0(1, near)
+
+    w_2(2, far)
+    w_1(1, near)
+
+    @pl.when(is_outer)
+    def _():
+        w_0(2, near)
+
+    w_1(2, near)
+
+    @pl.when(z == 2)
+    def _():
+        chain_pass(3)
+
+    w_3(1, far)
+    w_3(2, far)
+
+    @pl.when(is_outer)
+    def _():
+        w_0(1, mid)
+
+    w_1(1, mid)
+
+    @pl.when(is_outer)
+    def _():
+        w_0(2, mid)
+
+    w_1(2, mid)
 
     def p1b(g, _):
         @pl.when(z == NT - 1)
@@ -629,11 +765,8 @@
         return 0
 
     lax.fori_loop(0, NT, p1c, 0)
-    for k in (1, 2):
-        w_1(k, mid)
-    for k in (1, 2):
-        w_3(k, near)
-        w_2(k, far)
+    w_2(1, near)
+    w_2(2, near)
 
     def p2(n, _):
         acc = None
@@ -654,8 +787,8 @@
         return 0
 
     lax.fori_loop(0, T // 128, p2b, 0)
-    w_3(1, far)
-    w_3(2, far)
+    w_3(1, near)
+    w_3(2, near)
 
     @pl.when(z < NT - 1)
     def _():
@@ -664,7 +797,7 @@
 
     UN[...] = jnp.zeros_like(UN)
     GN2[...] = jnp.zeros_like(GN2)
-    for copy in local[3:]:
+    for copy in local[4:]:
         copy.wait()
 
     cc = math.sqrt(2.0 / math.pi)
@@ -678,7 +811,7 @@
             w_4(2, g)
 
         def units(u, total):
-            pre = dot(N2[...], WB[g, :, col(u)]) + BP[g, pl.ds(1, 1), col(u)]
+            pre = dot(N2[...], WB[g, :, col(u)]) + BP[g, pl.ds(3, 1), col(u)]
             sq = pre * pre
             t = jnp.tanh(cc * pre * (1.0 + 0.044715 * sq))
             act = (0.5 * pre * (1.0 + t)).astype(BF)
@@ -915,7 +1048,7 @@
         for which, parts in ((0, gql), (1, gkl)):
             glog = jnp.concatenate(parts, axis=0)
             own = QK[g, pl.ds(which * HC, HC), :]
-            GQ[pl.ds(which * HC, HC), :] = dot(block_diag(g, which), glog, 0, 0).astype(BF)
+            GQ[pl.ds(which * HC, HC), :] = dot(block_diag(g, which), glog).astype(BF)
             gfeat = jnp.where(head_mask, dot(own, glog, 1, 1), 0.0).astype(BF)
             part = dot(gfeat, pick_back(which))
             comp = part if comp is None else comp + part
@@ -1017,16 +1150,34 @@
     o_3(1)
     o_3(2)
     o_2(0)
-    outs = [o_4(1, ob_ref, own_s.at[0]), o_4(2, oc_ref, own_s.at[1])]
+    o_4(1)
+    outs = [*out_ff(1, MID, 0, ob_ref, 0)]
+    o_4(2)
+    outs += [*out_ff(2, UN, 1, oc_ref, 2)]
     for o in range(1, NT):
         zz = lax.rem(z + o, NT)
         rcopy(LZ.at[zz], LZ.at[zz], lz_s.at[o - 1], lz_r.at[zz], (dp, z)).wait_recv()
     total = LZ[0]
     for zz in range(1, NT):
         total = total + LZ[zz]
-    ov_ref[...] = total
+    gln1g_ref[...] = total[0:1].reshape(D)
+    gln1b_ref[...] = total[1:2].reshape(D)
     o_3(0)
-    outs.append(o_4(0, oa_ref, own_s.at[2]))
+    o_4(0)
+    widen(OA, 0, WO, 0, QKV)
+    outs.append(write(WO.at[pl.ds(0, QKV), :], oa_ref, own_s.at[4]))
+    widen(OA, QKV, WO, QKV, HC)
+    outs.append(write(WO.at[pl.ds(QKV, HC), :], oo_ref, own_s.at[5]))
+    for b in range(HC // 32):
+        block = OA[D : D + 32, b * 128 : (b + 1) * 128].astype(F32)
+        rows = slice(b % 2 * 32, b % 2 * 32 + 32)
+        gfq_ref[b // 2, rows, :] = block[:, :HD]
+        gfk_ref[b // 2, rows, :] = block[:, HD:]
+    vec = OA[D + 32 : D + 48, :].astype(F32)
+    for i in range(3):
+        gbqkv_ref[i : i + 1, :] = vec[0:1, i * HC : (i + 1) * HC]
+    for i, ref in enumerate((gbfc_ref, gbproj_ref, gbout_ref, gln2g_ref, gln2b_ref)):
+        ref[...] = vec[i + 1 : i + 2].reshape(D)
     for copy in outs:
         copy.wait()
 
@@ -1093,9 +1244,13 @@
         vm((NH, AUG, 2 * HD), F32),
         vm((D, T)),
         vm((4, 1, D), F32),
+        vm((6, 1, D), F32),
+        vm((HC, 2 * HD)),
+        vm((8, D), F32),
+        vm((D, D), F32),
     ]
     scratch += [
-        dma((5,)),
+        dma((6,)),
         dma((2, NT - 1)),
         dma((2, NT)),
         dma((KINDS, 2)),
@@ -1122,13 +1277,17 @@
         out_shape=(
             jax.ShapeDtypeStruct((T, D), BF),
             jax.ShapeDtypeStruct((T, D), BF),
-            jax.ShapeDtypeStruct((ROWS_G[0], D), BF),
-            jax.ShapeDtypeStruct((D, U), BF),
-            jax.ShapeDtypeStruct((U, D), BF),
-            jax.ShapeDtypeStruct((8, D), F32),
+            jax.ShapeDtypeStruct((QKV, D), F32),
+            jax.ShapeDtypeStruct((HC, D), F32),
+            jax.ShapeDtypeStruct((D, U), F32),
+            jax.ShapeDtypeStruct((U, D), F32),
+            jax.ShapeDtypeStruct((HPG, HD, HD), F32),
+            jax.ShapeDtypeStruct((HPG, HD, HD), F32),
+            jax.ShapeDtypeStruct((3, HC), F32),
+            *[jax.ShapeDtypeStruct((D,), F32)] * 7,
         ),
-        in_specs=[pl.BlockSpec(memory_space=pltpu.SMEM)] + [vmem] * 8 + [hbm] * 5,
-        out_specs=(vmem, vmem, hbm, hbm, hbm, vmem),
+        in_specs=[pl.BlockSpec(memory_space=pltpu.SMEM)] + [vmem] * 12 + [hbm] * 4,
+        out_specs=(vmem, vmem, hbm, hbm, hbm, hbm, *[vmem] * 10),
         scratch_shapes=scratch,
         compiler_params=pltpu.CompilerParams(
             collective_id=0, has_side_effects=True, vmem_limit_bytes=67043328
@@ -1157,57 +1316,47 @@
     cotangent,
 ):
     T = tokens_in.shape[0]
-    a_own = jnp.concatenate([jnp.transpose(w_qkv, (1, 2, 0)).reshape(QKV, D), w_out], axis=0)
-    ft_own = jnp.concatenate(
-        [jnp.transpose(feat_q, (0, 2, 1)).reshape(HC, HD), jnp.transpose(feat_k, (0, 2, 1)).reshape(HC, HD)],
-        axis=1,
-    )
-    bq = jnp.pad(b_qkv.reshape(1, QKV), ((0, 0), (0, D - QKV)))
-    bp_own = jnp.concatenate([bq, b_fc.reshape(1, U), jnp.zeros((6, D), F32)], axis=0)
-
-    def row(v):
-        return v.reshape(1, D)
-
-    res, gin, oa, ob, oc, ov = layer_call(
+    w_qkv_t = jnp.transpose(w_qkv, (1, 2, 0)).reshape(QKV, D)
+    res, gin, g_w_qkv, g_w_out, g_w_fc, g_w_proj, g_fq, g_fk, g_bqkv, g_bfc, g_bproj, g_bout, *g_ln = layer_call(
         nh,
         T,
         seq_lengths,
         tokens_in,
         cotangent,
-        row(ln1_gain),
-        row(ln1_bias),
-        row(b_out),
-        row(ln2_gain),
-        row(ln2_bias),
-        row(b_proj),
-        a_own,
+        ln1_gain,
+        ln1_bias,
+        b_out,
+        ln2_gain,
+        ln2_bias,
+        b_proj,
+        b_fc,
+        b_qkv,
+        feat_q,
+        feat_k,
+        w_qkv_t,
+        w_out,
         w_fc,
         w_proj,
-        ft_own,
-        bp_own,
     )
-    g_w_qkv = jnp.transpose(oa[:QKV].reshape(3, HC, D), (2, 0, 1)).astype(F32)
-    g_w_out = oa[QKV:D].astype(F32)
-    feats = jnp.transpose(oa[D : D + 32].reshape(32, HC // 32, 2 * HD), (1, 0, 2)).reshape(HC, 2 * HD)
-    feats = feats.astype(F32).reshape(HPG, HD, 2 * HD)
-    vec = oa[D + 32 : D + 48].astype(F32)
+    g_w_qkv = jnp.transpose(g_w_qkv.reshape(3, HC, D), (2, 0, 1))
+    g_ln2g, g_ln2b, g_ln1g, g_ln1b = g_ln
     return (
         res,
         gin,
-        ov[0],
-        ov[1],
+        g_ln1g,
+        g_ln1b,
         g_w_qkv,
-        vec[0, :QKV].reshape(3, HC),
-        feats[:, :, :HD],
-        feats[:, :, HD:],
+        g_bqkv,
+        g_fq,
+        g_fk,
         g_w_out,
-        vec[3],
-        vec[4],
-        vec[5],
-        ob.astype(F32),
-        vec[1],
-        oc.astype(F32),
-        vec[2],
+        g_bout,
+        g_ln2g,
+        g_ln2b,
+        g_w_fc,
+        g_bfc,
+        g_w_proj,
+        g_bproj,
     )
 
 

time: 226 us -> 195 us (0.86)
  Pallas kernels: 196 us -> 179 us
  other arithmetic: 11.7 us -> 0 us
    pallas_call x1, Pallas kernels: 196 us -> 179 us  [layer_call(): pl.pallas_call(functools.partial(layer_kernel, nh), out_shape=(jax.ShapeD...]
    unnamed x12 -> x44, local copies, waits for them, and re-layouts: 2.76 us -> 15.7 us
    reshape x8 -> x0, local copies, waits for them, and re-layouts: 9.06 us -> none  [the longest x6 7.6 us: row(): return v.reshape(1, D)]
    convert_element_type x6 -> x0, other arithmetic: 7.97 us -> none  [the longest x1 1.81 us: local(): g_w_out = oa[QKV:D].astype(F32)]
    concatenate x3 -> x0, other arithmetic: 3.74 us -> none  [the longest x1 2.35 us: local(): jnp.concatenate([jnp.transpose(w_qkv, (1, 2, 0)).reshape(QKV, D), w_out],...]
    slice x4 -> x0, local copies, waits for them, and re-layouts: 2.3 us -> none  [the longest x1 1.49 us: local(): vec[2]]
where the time goes in v4:
time: 195 us
  Pallas kernels  179 us (92%)
  local copies, waits for them, and re-layouts  15.7 us (8%)
    pallas_call x1, Pallas kernels, layer_call(): pl.pallas_call(functools.partial(layer_kernel, nh), out_shape=(jax.ShapeD...  179 us
    unnamed x44, local copies, waits for them, and re-layouts  15.7 us

profile of v4, /device:TPU:1, one launch (start us, length us, event | category | flops | bytes accessed | tf_op | source)
XLA Modules:
  0.0 195.0 jit_solution(2490231670641805500)
XLA Ops:
  0.7 178.6 %shard_map.288 = (bf16[512,768]{1,0:T(8,128)(2,1)}, bf16[512,768]{1,0:T(8,128)(2,1)}, f32[576,768]{1,0:T(8,128)}, f32[192,768]{1,0:T(8,128)}, f32[768,768]{1,0:T...) custom-call(s32[1,2]{1,0:T(1,128)} %seq_ref.1, ...), custom_call_target="tpu_custom_call" | custom-call | tf_op jit(solution)/shard_map/pallas_call | solution.py:1275
  179.2 0.0 copy-start.13
  179.2 0.0 copy-start.12
  179.2 0.0 copy-start.2
  179.2 2.2 %copy.49 = bf16[512,768]{1,0:T(8,128)(2,1)} copy(bf16[512,768]{1,0:T(8,128)(2,1)} %get-tuple-element.64) | data formatting | bytes 1572864
  181.4 2.1 %copy.50 = bf16[512,768]{1,0:T(8,128)(2,1)} copy(bf16[512,768]{1,0:T(8,128)(2,1)} %get-tuple-element.65) | data formatting | bytes 1572864
  183.5 0.0 copy-done.13
  183.6 0.6 copy.51
  184.1 0.0 copy-done.12
  184.2 0.6 copy.52
  184.7 0.0 copy-done.2
  184.8 0.0 copy-start.1
  184.8 1.2 copy.53
  186.0 0.0 copy-done.11
  186.0 0.6 copy.54
  186.6 0.0 copy-done.5
  186.6 0.6 copy.55
  187.2 0.0 copy-done.4
  187.2 0.6 copy.56
  187.9 0.0 copy-done.3
  187.9 0.8 copy.57
  188.7 0.0 copy-done.10
  188.7 0.6 copy.58
  189.3 0.6 copy.59
  189.9 0.0 copy-done.8
  189.9 0.6 copy.60
  190.5 0.0 copy-done.1
  190.5 1.4 copy.61
  191.9 0.6 copy.62
  192.5 0.5 copy-done
  193.0 1.4 copy.63
  194.4 0.6 copy.64
  (13 shorter events, 0.0 us)
Async XLA Ops:
  179.2 4.3 %copy-start.13 = (f32[768]{0:T(1024)S(1)}, f32[768]{0:T(1024)}, u32[]{:S(2)}) copy-start(f32[768]{0:T(1024)} %get-tuple-element.66) | copy-start | bytes 9220
  179.2 4.9 %copy-start.12 = (f32[768]{0:T(1024)S(1)}, f32[768]{0:T(1024)}, u32[]{:S(2)}) copy-start(f32[768]{0:T(1024)} %get-tuple-element.67) | copy-start | bytes 9220
  179.2 5.5 %copy-start.2 = (f32[576,768]{1,0:T(8,128)S(1)}, f32[576,768]{1,0:T(8,128)}, u32[]{:S(2)}) copy-start(f32[576,768]{1,0:T(8,128)} %get-tuple-element.36) | copy-start | bytes 5308420
  181.4 4.5 %copy-start.11 = (f32[3,192]{1,0:T(4,128)S(1)}, f32[3,192]{1,0:T(4,128)}, u32[]{:S(2)}) copy-start(f32[3,192]{1,0:T(4,128)} %get-tuple-element.69) | copy-start | bytes 6916
  181.4 5.1 %copy-start.5 = (f32[3,64,64]{2,1,0:T(8,128)S(1)}, f32[3,64,64]{2,1,0:T(8,128)}, u32[]{:S(2)}) copy-start(f32[3,64,64]{2,1,0:T(8,128)} %get-tuple-element.70) | copy-start | bytes 147460
  181.4 5.8 %copy-start.4 = (f32[3,64,64]{2,1,0:T(8,128)S(1)}, f32[3,64,64]{2,1,0:T(8,128)}, u32[]{:S(2)}) copy-start(f32[3,64,64]{2,1,0:T(8,128)} %get-tuple-element.71) | copy-start | bytes 147460
  183.6 4.3 %copy-start.3 = (f32[192,768]{1,0:T(8,128)S(1)}, f32[192,768]{1,0:T(8,128)}, u32[]{:S(2)}) copy-start(f32[192,768]{1,0:T(8,128)} %get-tuple-element.72) | copy-start | bytes 1769476
  184.7 3.9 %copy-start.10 = (f32[768]{0:T(1024)S(1)}, f32[768]{0:T(1024)}, u32[]{:S(2)}) copy-start(f32[768]{0:T(1024)} %get-tuple-element.73) | copy-start | bytes 9220
  184.7 4.5 %copy-start.9 = (f32[768]{0:T(1024)S(1)}, f32[768]{0:T(1024)}, u32[]{:S(2)}) copy-start(f32[768]{0:T(1024)} %get-tuple-element.74) | copy-start | bytes 9220
  184.8 5.1 %copy-start.8 = (f32[768]{0:T(1024)S(1)}, f32[768]{0:T(1024)}, u32[]{:S(2)}) copy-start(f32[768]{0:T(1024)} %get-tuple-element.75) | copy-start | bytes 9220
  184.8 5.7 %copy-start.1 = (f32[768,768]{1,0:T(8,128)S(1)}, f32[768,768]{1,0:T(8,128)}, u32[]{:S(2)}) copy-start(f32[768,768]{1,0:T(8,128)} %get-tuple-element.76) | copy-start | bytes 7077892
  190.5 1.4 copy-start.7
  190.5 2.5 %copy-start = (f32[768,768]{1,0:T(8,128)S(1)}, f32[768,768]{1,0:T(8,128)}, u32[]{:S(2)}) copy-start(f32[768,768]{1,0:T(8,128)} %get-tuple-element.78) | copy-start | bytes 7077892
  193.0 1.4 copy-start.6

commit v5 on v4

--- a/solution.py
+++ b/solution.py
@@ -1295,6 +1295,33 @@
     )(*args)
 
 
+def hand_over(arrays):
+    n = len(arrays)
+
+    def body(*refs):
+        sems = refs[3 * n]
+
+        def move(a, b, i):
+            return pltpu.make_async_copy(refs[a * n + i], refs[b * n + i], sems.at[b % 2, i])
+
+        for i in range(n):
+            move(0, 2, i).start()
+        for i in range(n):
+            move(0, 2, i).wait()
+            move(2, 1, i).start()
+        for i in range(n):
+            move(2, 1, i).wait()
+
+    hbm = pl.BlockSpec(memory_space=pl.ANY)
+    return pl.pallas_call(
+        body,
+        out_shape=tuple(jax.ShapeDtypeStruct(a.shape, a.dtype) for a in arrays),
+        in_specs=[hbm] * len(arrays),
+        out_specs=(hbm,) * len(arrays),
+        scratch_shapes=[*[pltpu.VMEM(a.shape, a.dtype) for a in arrays], pltpu.SemaphoreType.DMA((2, n))],
+    )(*arrays)
+
+
 def local(
     nh,
     tokens_in,
@@ -1317,7 +1344,7 @@
 ):
     T = tokens_in.shape[0]
     w_qkv_t = jnp.transpose(w_qkv, (1, 2, 0)).reshape(QKV, D)
-    res, gin, g_w_qkv, g_w_out, g_w_fc, g_w_proj, g_fq, g_fk, g_bqkv, g_bfc, g_bproj, g_bout, *g_ln = layer_call(
+    out = layer_call(
         nh,
         T,
         seq_lengths,
@@ -1338,6 +1365,7 @@
         w_fc,
         w_proj,
     )
+    res, gin, g_w_qkv, g_w_out, g_w_fc, g_w_proj, g_fq, g_fk, g_bqkv, g_bfc, g_bproj, g_bout, *g_ln = hand_over(out)
     g_w_qkv = jnp.transpose(g_w_qkv.reshape(3, HC, D), (2, 0, 1))
     g_ln2g, g_ln2b, g_ln1g, g_ln1b = g_ln
     return (

time: 195 us -> 186 us (0.954)
  local copies, waits for them, and re-layouts: 15.7 us -> 0 us
  Pallas kernels: 179 us -> 185 us
    unnamed x44 -> x0, local copies, waits for them, and re-layouts: 15.7 us -> none
    pallas_call x0 -> x1, Pallas kernels: none -> 6.84 us  [hand_over(): pl.pallas_call(body, out_shape=tuple((jax.ShapeDtypeStruct(a.shape, a.dty...]
where the time goes in v5:
time: 186 us
  Pallas kernels  185 us (99%)
    pallas_call x1, Pallas kernels, layer_call(): pl.pallas_call(functools.partial(layer_kernel, nh), out_shape=(jax.ShapeD...  179 us
    pallas_call x1, Pallas kernels, hand_over(): pl.pallas_call(body, out_shape=tuple((jax.ShapeDtypeStruct(a.shape, a.dty...  6.84 us

profile of v5, /device:TPU:1, one launch (start us, length us, event | category | flops | bytes accessed | tf_op | source)
XLA Modules:
  0.0 186.2 jit_solution(442108088827278957)
XLA Ops:
  0.7 178.5 %shard_map.288 = (bf16[512,768]{1,0:T(8,128)(2,1)}, bf16[512,768]{1,0:T(8,128)(2,1)}, f32[576,768]{1,0:T(8,128)}, f32[192,768]{1,0:T(8,128)}, f32[768,768]{1,0:T...) custom-call(s32[1,2]{1,0:T(1,128)} %seq_ref.1, ...), custom_call_target="tpu_custom_call" | custom-call | tf_op jit(solution)/shard_map/pallas_call | solution.py:1275
  179.2 6.8 %shard_map.289 = (bf16[512,768]{1,0:T(8,128)(2,1)}, bf16[512,768]{1,0:T(8,128)(2,1)}, f32[576,768]{1,0:T(8,128)}, f32[192,768]{1,0:T(8,128)}, f32[768,768]{1,0:T...) custom-call(bf16[512,768]{1,0:T(8,128)(2,1)} %get-tuple-element.48.r, ...), custom_call_target="tpu_custom_call" | custom-call | tf_op jit(solution)/shard_map/pallas_call | solution.py:1316

commit v6 on v4

--- a/solution.py
+++ b/solution.py
@@ -151,7 +151,6 @@
     PV,
     ft_own,
     bp_own,
-    WO,
     own_s,
     sm_s,
     sm_r,
@@ -486,35 +485,26 @@
         o_send(k, 2, ohalf(k, slot_x, 0), dev_y)
         o_wait(k, 1, orows(k, slot_y))
         o_send(k, 3, ohalf(k, slot_y, 1), dev_x)
+        for i, s in enumerate((slot, slot_x, slot_y)):
+            o_send(k, 4 + i, orows(k, s), dev_c)
 
     def o_3(k):
         o_wait(k, 2, ohalf(k, slot_d, 0))
         o_wait(k, 3, ohalf(k, slot_d, 1))
-        o_send(k, 4, orows(k, core * 4, 4), dev_c)
+        o_send(k, 7, orows(k, slot_d), dev_c)
 
     def o_4(k):
-        o_wait(k, 4, orows(k, (1 - core) * 4, 4))
-        sent = [orows(k, slot)] * 2 + [ohalf(k, slot_x, 0), ohalf(k, slot_y, 1), orows(k, core * 4, 4)]
+        slots = (slot, slot_x, slot_y, slot_d)
+        for i, s in enumerate(slots):
+            o_wait(k, 4 + i, orows(k, s + (1 - 2 * core) * 4))
+        sent = [orows(k, slot)] * 2 + [ohalf(k, slot_x, 0), ohalf(k, slot_y, 1)] + [orows(k, s) for s in slots]
         for st, ref in enumerate(sent):
             rcopy(ref, ref, o_s.at[st, k], o_r.at[0, k], dev_c).wait_send()
-
-    def widen(src, start, dst, first, n):
-        def body(i, _):
-            dst[pl.ds(mo(first + i * 64, 64), 64), :] = src[pl.ds(mo(start + i * 64, 64), 64), :].astype(F32)
-            return 0
-
-        lax.fori_loop(0, n // 64, body, 0)
 
     def write(src, dst, sem):
         copy = pltpu.make_async_copy(src, dst, sem)
         copy.start()
         return copy
-
-    def out_ff(k, big, part, out, sem):
-        widen(O[k], 0, big, 0, T)
-        first = write(big, out.at[pl.ds(0, T), :], own_s.at[sem])
-        widen(O[k], T, GN2, part * (D - T), D - T)
-        return first, write(GN2.at[pl.ds(part * (D - T), D - T), :], out.at[pl.ds(T, D - T), :], own_s.at[sem + 1])
 
     def iota(shape, axis):
         return lax.broadcasted_iota(jnp.int32, shape, axis)
@@ -697,6 +687,10 @@
         return 0
 
     lax.fori_loop(0, NT, p1, 0)
+    @pl.when(is_inner)
+    def _():
+        w_0(2, mid)
+
     w_2(1, far)
 
     @pl.when(z == 1)
@@ -708,10 +702,6 @@
         chain_pass(0)
         chain_pass(2)
 
-    @pl.when(is_inner)
-    def _():
-        w_0(2, mid)
-
     @pl.when(is_outer)
     def _():
         w_0(1, near)
@@ -728,21 +718,6 @@
     @pl.when(z == 2)
     def _():
         chain_pass(3)
-
-    w_3(1, far)
-    w_3(2, far)
-
-    @pl.when(is_outer)
-    def _():
-        w_0(1, mid)
-
-    w_1(1, mid)
-
-    @pl.when(is_outer)
-    def _():
-        w_0(2, mid)
-
-    w_1(2, mid)
 
     def p1b(g, _):
         @pl.when(z == NT - 1)
@@ -765,8 +740,8 @@
         return 0
 
     lax.fori_loop(0, NT, p1c, 0)
-    w_2(1, near)
-    w_2(2, near)
+    w_3(1, far)
+    w_3(2, far)
 
     def p2(n, _):
         acc = None
@@ -787,8 +762,16 @@
         return 0
 
     lax.fori_loop(0, T // 128, p2b, 0)
-    w_3(1, near)
-    w_3(2, near)
+    for k in (1, 2):
+
+        @pl.when(is_outer)
+        def _():
+            w_0(k, mid)
+
+        w_1(k, mid)
+
+    w_2(1, near)
+    w_2(2, near)
 
     @pl.when(z < NT - 1)
     def _():
@@ -833,6 +816,8 @@
 
         @pl.when(j == 1)
         def _():
+            w_3(1, near)
+            w_3(2, near)
             w_3(1, mid)
             w_3(2, mid)
 
@@ -1151,9 +1136,9 @@
     o_3(2)
     o_2(0)
     o_4(1)
-    outs = [*out_ff(1, MID, 0, ob_ref, 0)]
+    outs = [write(OB, ob_ref, own_s.at[0])]
     o_4(2)
-    outs += [*out_ff(2, UN, 1, oc_ref, 2)]
+    outs.append(write(OC, oc_ref, own_s.at[1]))
     for o in range(1, NT):
         zz = lax.rem(z + o, NT)
         rcopy(LZ.at[zz], LZ.at[zz], lz_s.at[o - 1], lz_r.at[zz], (dp, z)).wait_recv()
@@ -1164,10 +1149,8 @@
     gln1b_ref[...] = total[1:2].reshape(D)
     o_3(0)
     o_4(0)
-    widen(OA, 0, WO, 0, QKV)
-    outs.append(write(WO.at[pl.ds(0, QKV), :], oa_ref, own_s.at[4]))
-    widen(OA, QKV, WO, QKV, HC)
-    outs.append(write(WO.at[pl.ds(QKV, HC), :], oo_ref, own_s.at[5]))
+    outs.append(write(OA.at[pl.ds(0, QKV), :], oa_ref, own_s.at[4]))
+    outs.append(write(OA.at[pl.ds(QKV, HC), :], oo_ref, own_s.at[5]))
     for b in range(HC // 32):
         block = OA[D : D + 32, b * 128 : (b + 1) * 128].astype(F32)
         rows = slice(b % 2 * 32, b % 2 * 32 + 32)
@@ -1247,7 +1230,6 @@
         vm((6, 1, D), F32),
         vm((HC, 2 * HD)),
         vm((8, D), F32),
-        vm((D, D), F32),
     ]
     scratch += [
         dma((6,)),
@@ -1259,8 +1241,8 @@
         dma((6, KINDS, NT)),
         dma((5, KINDS, NT)),
         dma((KINDS, NT + 1)),
-        dma((5, KINDS)),
-        dma((5, KINDS)),
+        dma((8, KINDS)),
+        dma((8, KINDS)),
         dma((nhb, KINDS)),
         dma((nhb, KINDS)),
         dma((nst,)),
@@ -1277,10 +1259,10 @@
         out_shape=(
             jax.ShapeDtypeStruct((T, D), BF),
             jax.ShapeDtypeStruct((T, D), BF),
-            jax.ShapeDtypeStruct((QKV, D), F32),
-            jax.ShapeDtypeStruct((HC, D), F32),
-            jax.ShapeDtypeStruct((D, U), F32),
-            jax.ShapeDtypeStruct((U, D), F32),
+            jax.ShapeDtypeStruct((QKV, D), BF),
+            jax.ShapeDtypeStruct((HC, D), BF),
+            jax.ShapeDtypeStruct((D, U), BF),
+            jax.ShapeDtypeStruct((U, D), BF),
             jax.ShapeDtypeStruct((HPG, HD, HD), F32),
             jax.ShapeDtypeStruct((HPG, HD, HD), F32),
             jax.ShapeDtypeStruct((3, HC), F32),
@@ -1293,6 +1275,48 @@
             collective_id=0, has_side_effects=True, vmem_limit_bytes=67043328
         ),
     )(*args)
+
+
+def hand_over(arrays):
+    n = len(arrays)
+    wide = (2, 3, 4, 5)
+    order = (4, 5, *(i for i in range(n) if i not in wide), 2, 3)
+    kinds = [F32 if i in wide else a.dtype for i, a in enumerate(arrays)]
+
+    def body(*refs):
+        taken, given, low = refs[:n], refs[n : 2 * n], refs[2 * n : 3 * n]
+        high = dict(zip(wide, refs[3 * n : 3 * n + len(wide)]))
+        sems = refs[3 * n + len(wide)]
+
+        def widen(src, dst):
+            def step(i, _):
+                at = pl.ds(mo(i * 64, 64), 64)
+                dst[at, :] = src[at, :].astype(F32)
+                return 0
+
+            lax.fori_loop(0, src.shape[0] // 64, step, 0)
+
+        reads = [pltpu.make_async_copy(taken[i], low[i], sems.at[0, i]) for i in range(n)]
+        writes = [pltpu.make_async_copy(high.get(i, low[i]), given[i], sems.at[1, i]) for i in range(n)]
+        for i in order:
+            reads[i].start()
+        for i in order:
+            reads[i].wait()
+            if i in wide:
+                widen(low[i], high[i])
+            writes[i].start()
+        for i in order:
+            writes[i].wait()
+
+    hbm = pl.BlockSpec(memory_space=pl.ANY)
+    scratch = [pltpu.VMEM(a.shape, a.dtype) for a in arrays] + [pltpu.VMEM(arrays[i].shape, F32) for i in wide]
+    return pl.pallas_call(
+        body,
+        out_shape=tuple(jax.ShapeDtypeStruct(a.shape, kind) for a, kind in zip(arrays, kinds)),
+        in_specs=[hbm] * n,
+        out_specs=(hbm,) * n,
+        scratch_shapes=[*scratch, pltpu.SemaphoreType.DMA((2, n))],
+    )(*arrays)
 
 
 def local(
@@ -1317,7 +1341,7 @@
 ):
     T = tokens_in.shape[0]
     w_qkv_t = jnp.transpose(w_qkv, (1, 2, 0)).reshape(QKV, D)
-    res, gin, g_w_qkv, g_w_out, g_w_fc, g_w_proj, g_fq, g_fk, g_bqkv, g_bfc, g_bproj, g_bout, *g_ln = layer_call(
+    out = layer_call(
         nh,
         T,
         seq_lengths,
@@ -1338,6 +1362,7 @@
         w_fc,
         w_proj,
     )
+    res, gin, g_w_qkv, g_w_out, g_w_fc, g_w_proj, g_fq, g_fk, g_bqkv, g_bfc, g_bproj, g_bout, *g_ln = hand_over(out)
     g_w_qkv = jnp.transpose(g_w_qkv.reshape(3, HC, D), (2, 0, 1))
     g_ln2g, g_ln2b, g_ln1g, g_ln1b = g_ln
     return (

time: 195 us -> 180 us (0.923)
  local copies, waits for them, and re-layouts: 15.7 us -> 0 us
    unnamed x44 -> x0, local copies, waits for them, and re-layouts: 15.7 us -> none
    pallas_call x0 -> x1, Pallas kernels: none -> 5.25 us  [hand_over(): pl.pallas_call(body, out_shape=tuple((jax.ShapeDtypeStruct(a.shape, kind)...]
    pallas_call x1, Pallas kernels: 179 us -> 174 us  [layer_call(): pl.pallas_call(functools.partial(layer_kernel, nh), out_shape=(jax.ShapeD...]
where the time goes in v6:
time: 180 us
  Pallas kernels  179 us (99%)
    pallas_call x1, Pallas kernels, layer_call(): pl.pallas_call(functools.partial(layer_kernel, nh), out_shape=(jax.ShapeD...  174 us
    pallas_call x1, Pallas kernels, hand_over(): pl.pallas_call(body, out_shape=tuple((jax.ShapeDtypeStruct(a.shape, kind)...  5.25 us

profile of v6, /device:TPU:1, one launch (start us, length us, event | category | flops | bytes accessed | tf_op | source)
XLA Modules:
  0.0 179.7 jit_solution(8841453746432751206)
XLA Ops:
  0.7 173.6 %shard_map.288 = (bf16[512,768]{1,0:T(8,128)(2,1)}, bf16[512,768]{1,0:T(8,128)(2,1)}, bf16[576,768]{1,0:T(8,128)(2,1)}, bf16[192,768]{1,0:T(8,128)(2,1)}, bf16[7...) custom-call(s32[1,2]{1,0:T(1,128)} %seq_ref.1, ...), custom_call_target="tpu_custom_call" | custom-call | tf_op jit(solution)/shard_map/pallas_call | solution.py:1257
  174.3 5.2 %shard_map.289 = (bf16[512,768]{1,0:T(8,128)(2,1)}, bf16[512,768]{1,0:T(8,128)(2,1)}, f32[576,768]{1,0:T(8,128)}, f32[192,768]{1,0:T(8,128)}, f32[768,768]{1,0:T...) custom-call(bf16[512,768]{1,0:T(8,128)(2,1)} %get-tuple-element.48.r, ...), custom_call_target="tpu_custom_call" | custom-call | tf_op jit(solution)/shard_map/pallas_call | solution.py:1313

commit v7 on v6

--- a/solution.py
+++ b/solution.py
@@ -305,15 +305,20 @@
         w_send(k, g, 2, 3, whalf(k, g, slot_x, 0), dev_y)
         w_wait(k, g, 2, wrows(k, g, slot_y))
         w_send(k, g, 3, 4, whalf(k, g, slot_y, 1), dev_x)
+        for i, s in enumerate((slot, slot_x, slot_y)):
+            w_send(k, g, 6 + i, 5 + i, wrows(k, g, s), dev_c)
 
     def w_3(k, g):
         w_wait(k, g, 3, whalf(k, g, slot_d, 0))
         w_wait(k, g, 4, whalf(k, g, slot_d, 1))
-        w_send(k, g, 4, 5, wrows4(k, g, core), dev_c)
+        w_send(k, g, 4, 8, wrows(k, g, slot_d), dev_c)
 
     def w_4(k, g):
-        w_wait(k, g, 5, wrows4(k, g, 1 - core))
-        sent = [wrows(k, g, slot)] * 2 + [whalf(k, g, slot_x, 0), whalf(k, g, slot_y, 1), wrows4(k, g, core)]
+        for i, s in enumerate((slot, slot_x, slot_y, slot_d)):
+            w_wait(k, g, 5 + i, wrows(k, g, s + (1 - 2 * core) * 4))
+        for i in range(3):
+            rcopy(wrows(k, g, slot), wrows(k, g, slot), w_s.at[6 + i, k, g], w_r.at[0, k, g], dev_c).wait_send()
+        sent = [wrows(k, g, slot)] * 2 + [whalf(k, g, slot_x, 0), whalf(k, g, slot_y, 1), wrows(k, g, slot_d)]
         for st, ref in enumerate(sent):
             rcopy(ref, ref, w_s.at[st, k, g], w_r.at[0, k, g], dev_c).wait_send()
 
@@ -1236,8 +1241,8 @@
         dma((2, NT - 1)),
         dma((2, NT)),
         dma((KINDS, 2)),
-        dma((6, KINDS, NT)),
-        dma((6, KINDS, NT)),
+        dma((9, KINDS, NT)),
+        dma((9, KINDS, NT)),
         dma((6, KINDS, NT)),
         dma((5, KINDS, NT)),
         dma((KINDS, NT + 1)),

time: 180 us -> 179 us (level)
  no operation moved by 1% of the time
where the time goes in v7:
time: 179 us
  Pallas kernels  178 us (99%)
    pallas_call x1, Pallas kernels, layer_call(): pl.pallas_call(functools.partial(layer_kernel, nh), out_shape=(jax.ShapeD...  172 us
    pallas_call x1, Pallas kernels, hand_over(): pl.pallas_call(body, out_shape=tuple((jax.ShapeDtypeStruct(a.shape, kind)...  5.25 us

profile of v7, /device:TPU:1, one launch (start us, length us, event | category | flops | bytes accessed | tf_op | source)
XLA Modules:
  0.0 178.6 jit_solution(14351598844078082518)
XLA Ops:
  0.7 172.5 %shard_map.288 = (bf16[512,768]{1,0:T(8,128)(2,1)}, bf16[512,768]{1,0:T(8,128)(2,1)}, bf16[576,768]{1,0:T(8,128)(2,1)}, bf16[192,768]{1,0:T(8,128)(2,1)}, bf16[7...) custom-call(s32[1,2]{1,0:T(1,128)} %seq_ref.1, ...), custom_call_target="tpu_custom_call" | custom-call | tf_op jit(solution)/shard_map/pallas_call | solution.py:1262
  173.2 5.2 %shard_map.289 = (bf16[512,768]{1,0:T(8,128)(2,1)}, bf16[512,768]{1,0:T(8,128)(2,1)}, f32[576,768]{1,0:T(8,128)}, f32[192,768]{1,0:T(8,128)}, f32[768,768]{1,0:T...) custom-call(bf16[512,768]{1,0:T(8,128)(2,1)} %get-tuple-element.48.r, ...), custom_call_target="tpu_custom_call" | custom-call | tf_op jit(solution)/shard_map/pallas_call | solution.py:1318
